TPU v7x, 128 devices: a whole 4x4x4 slice. The times are simulated.
128 devices in a mesh: dp: 16 (over y, x), tensor: 8 (over z, core).
Axes of the slice: x: 4, y: 4, z: 4, core: 2. Of those that a mesh axis runs over, the one named last changes fastest.
Arguments:
- tokens: bfloat16 [16384, 1536], P('dp'), may hold values from -6 to 6
- teacher_feats: bfloat16 [16384, 256], P('dp'), may hold values from -12 to 12
- masks: int32 [64, 256], P('dp'), may hold values from 0 to 1, as said below
- w_in: bfloat16 [1536, 2048], P('dp'), may hold values from -0.15625 to 0.15625
- w_out: bfloat16 [2048, 256], P('dp'), may hold values from -0.125 to 0.125
- proto_student: bfloat16 [256, 131072], P(None, ('dp', 'tensor')), may hold values from -0.375 to 0.375
- proto_teacher: bfloat16 [256, 131072], P(None, ('dp', 'tensor')), may hold values from -1 to 1
Outputs:
- d_tokens: bfloat16 [16384, 1536], P('dp')
- grad_in: float32 [1536, 2048], P('dp')
- grad_out: float32 [2048, 256], P('dp')
- grad_proto: float32 [256, 131072], P(None, ('dp', 'tensor'))
- crop_loss: float32 [64], P('dp')
Inputs may be any that keep to these rules, and one draw needn't show every extreme that they name: `masks`: the crops of one index of dp hold 256 or fewer masked patches together, exactly 256 on some index; a crop holds at most 129.
All inputs are finite; a program needn't handle non-finite values.
Results may differ from a plain program's by a relative error of at most 0.02.
Values may be sent and summed in bfloat16 or wider, within the bound.
No kernel may reach another device: no remote copies, remote signals or barrier semaphores. Data moves between devices by JAX's collectives and lax.ppermute only.
A program may use at most 192 MiB of HBM per device.

v0:
```python
import jax
import jax.numpy as jnp
from jax import lax
from jax.sharding import PartitionSpec as P

ROUNDS = 3
CAP = 256


TEACHER_TEMP = 0.07
STUDENT_TEMP = 0.1
EPS = 1e-06
GRAD_SCALE = 65536.0


def side_by_side(arrays, axis, dim, along):
    both = jnp.concatenate(arrays, axis=along)
    filled, at, outs = (lax.all_gather(both, axis, axis=dim, tiled=True), 0, [])
    for a in arrays:
        outs.append(lax.slice_in_dim(filled, at, at + a.shape[along], axis=along))
        at += a.shape[along]
    return tuple(outs)


def sent_to_all(x, axis):
    copies = jnp.broadcast_to(x, (lax.axis_size(axis), *x.shape))
    return lax.all_to_all(copies, axis, split_axis=0, concat_axis=0, tiled=True)


def taken_together(x, axis):
    return sent_to_all(x, axis).sum(axis=0)


def split_up(x, dim, peers):
    lengths = x.shape
    pieces = x.reshape(*lengths[:dim], peers, lengths[dim] // peers, *lengths[dim + 1 :])
    return jnp.moveaxis(pieces, dim, 0)


def sum_packed(arrays, axis, dims):
    peers = lax.axis_size(axis)
    pieces = [split_up(a, dim, peers) for a, dim in zip(arrays, dims)]
    lines = jnp.concatenate([b.reshape(peers, -1) for b in pieces], axis=1)
    width = max(16, -(-lines.shape[1] // 1024) * 8)
    lines = jnp.pad(lines, ((0, 0), (0, width * 128 - lines.shape[1]))).reshape(-1, 128)
    vector, at, outs = (lax.psum_scatter(lines, axis, tiled=True).reshape(-1), 0, [])
    for b in pieces:
        part = b[0]
        outs.append(vector[at : at + part.size].reshape(part.shape))
        at += part.size
    return tuple(outs)


def gelu_parts(pre):
    cdf = 0.5 * (1.0 + lax.erf(pre * 0.7071067811865476))
    pdf = jnp.exp(-0.5 * pre * pre) * 0.3989422804014327
    return (pre * cdf, cdf + pre * pdf)


def unit_rows(feats):
    inverse = lax.rsqrt(jnp.sum(feats * feats, axis=1, keepdims=True) + EPS)
    return (feats * inverse, inverse)


def unit_columns(protos):
    wide = protos.astype(jnp.float32)
    norms = jnp.sqrt(jnp.sum(wide * wide, axis=0, keepdims=True) + EPS)
    return (wide / norms, norms)


def head_forward(rows, teacher_pick, w_in_all, w_out_all):
    pre = jnp.dot(rows, w_in_all, preferred_element_type=jnp.float32)
    act, slope = gelu_parts(pre)
    hidden = act.astype(jnp.bfloat16)
    feats = jnp.dot(hidden, w_out_all, preferred_element_type=jnp.float32)
    unit, inv = unit_rows(feats)
    teacher_unit, _ = unit_rows(teacher_pick.astype(jnp.float32))
    return (hidden, slope, unit, inv, unit.astype(jnp.bfloat16), teacher_unit.astype(jnp.bfloat16))


def prototype_terms(
    student_rows,
    teacher_rows,
    student_cols,
    teacher_cols,
    live,
    weight,
    col_total,
    row_total,
    last_total,
):
    teacher_cos = jnp.dot(teacher_rows, teacher_cols, preferred_element_type=jnp.float32)
    expo = jnp.exp(teacher_cos / TEACHER_TEMP) * live[:, None]
    scores = jnp.dot(student_rows, student_cols, preferred_element_type=jnp.float32) / STUDENT_TEMP
    raised = jnp.exp(scores)
    scale_row = live
    for turn in range(ROUNDS):
        col_scale = 1.0 / col_total(jnp.sum(expo * scale_row[:, None], axis=0))
        balanced = expo * col_scale[None, :]
        if turn + 1 < ROUNDS:
            row_sum = row_total(jnp.sum(balanced, axis=1))
            scale_row = live / (row_sum + 1.0 - live)
    row_sum, norm_sum, cross = last_total(
        (jnp.sum(balanced, axis=1), jnp.sum(raised, axis=1), jnp.sum(balanced * scores, axis=1))
    )
    scale_row = live / (row_sum + 1.0 - live)
    row_loss = jnp.log(norm_sum) - scale_row * cross
    probs = raised / norm_sum[:, None]
    target = balanced * scale_row[:, None]
    grad_score = (weight[:, None] * (probs - target) / STUDENT_TEMP).astype(jnp.bfloat16)
    grad_part = lax.dot_general(
        grad_score, student_cols, (((1,), (1,)), ((), ())), preferred_element_type=jnp.float32
    )
    return (row_loss, grad_score, grad_part)


def head_backward(rows, hidden, slope, unit, inv, grad_unit, w_in_all, w_out_all):
    inner = jnp.sum(unit * grad_unit, axis=1, keepdims=True)
    grad_feats = (inv * (grad_unit - unit * inner)).astype(jnp.bfloat16)
    grad_out_part = lax.dot_general(
        hidden, grad_feats, (((0,), (0,)), ((), ())), preferred_element_type=jnp.float32
    )
    grad_hidden = lax.dot_general(
        grad_feats, w_out_all, (((1,), (1,)), ((), ())), preferred_element_type=jnp.float32
    )
    grad_pre = (grad_hidden * slope).astype(jnp.bfloat16)
    grad_in_part = lax.dot_general(
        rows, grad_pre, (((0,), (0,)), ((), ())), preferred_element_type=jnp.float32
    )
    grad_rows = lax.dot_general(
        grad_pre, w_in_all, (((1,), (1,)), ((), ())), preferred_element_type=jnp.float32
    )
    return (grad_in_part, grad_out_part, grad_rows)


def shards(tokens, teacher_feats, masks, w_in, w_out, proto_student, proto_teacher):
    crops, patches = masks.shape
    flat = masks.reshape(-1)
    index = jnp.nonzero(flat, size=CAP, fill_value=0)[0].astype(jnp.int32)
    live_own = (jnp.arange(CAP) < jnp.sum(flat)).astype(jnp.float32)
    inverse = 1.0 / jnp.maximum(jnp.sum(masks, axis=1), 1).astype(jnp.float32)
    member = (index[:, None] // patches == jnp.arange(crops)[None, :]).astype(
        jnp.float32
    ) * live_own[:, None]
    weight = (GRAD_SCALE * jnp.sum(member * inverse[None, :], axis=1)).astype(jnp.bfloat16)
    rows = jnp.take(tokens, index, axis=0)
    teacher_pick = jnp.take(teacher_feats, index, axis=0)
    s_cols, s_norm = unit_columns(proto_student)
    t_cols, _ = unit_columns(proto_teacher)
    s_cols_b = s_cols.astype(jnp.bfloat16)
    t_cols_b = t_cols.astype(jnp.bfloat16)
    w_in_all, w_out_all, student_all, teacher_all = (
        lax.all_gather(w_in, "dp", axis=0, tiled=True),
        lax.all_gather(w_out, "dp", axis=0, tiled=True),
        *side_by_side((s_cols_b, t_cols_b), "dp", 1, 0),
    )
    hidden, slope, unit, inv, student_rows, teacher_rows = head_forward(
        rows, teacher_pick, w_in_all, w_out_all
    )

    def col_total(values):
        return taken_together(values, "dp")

    def row_total(values):
        return taken_together(values, "tensor")

    def last_total(values):
        return jax.tree.map(lambda part: taken_together(part, "tensor"), values)

    row_loss, grad_score, grad_part = prototype_terms(
        student_rows,
        teacher_rows,
        student_all,
        teacher_all,
        live_own,
        weight.astype(jnp.float32),
        col_total,
        row_total,
        last_total,
    )
    grad_unit = taken_together(grad_part, "tensor")
    grad_cols_part = lax.dot_general(
        student_rows, grad_score, (((0,), (0,)), ((), ())), preferred_element_type=jnp.float32
    )
    grad_in_part, grad_out_part, grad_rows = head_backward(
        rows, hidden, slope, unit, inv, grad_unit, w_in_all, w_out_all
    )
    grad_in, grad_out, grad_cols = tuple(
        (
            part.astype(jnp.float32)
            for part in sum_packed(
                (
                    grad_in_part.astype(jnp.bfloat16),
                    grad_out_part.astype(jnp.bfloat16),
                    grad_cols_part.astype(jnp.bfloat16),
                ),
                "dp",
                (0, 0, 1),
            )
        )
    )
    grad_proto = (grad_cols - s_cols * jnp.sum(s_cols * grad_cols, axis=0, keepdims=True)) / s_norm
    crop_loss = jnp.sum(member * row_loss[:, None], axis=0) * inverse
    placed = (
        jnp.zeros((crops * patches, tokens.shape[1]), jnp.float32)
        .at[index]
        .add(grad_rows * live_own[:, None])
    )
    d_tokens = placed.astype(jnp.bfloat16)
    return (d_tokens, grad_in, grad_out, grad_proto, crop_loss)


def solution(mesh):
    placed = (
        P("dp", None),
        P("dp", None),
        P("dp", None),
        P("dp", None),
        P("dp", None),
        P(None, ("dp", "tensor")),
        P(None, ("dp", "tensor")),
    )
    return jax.shard_map(
        shards,
        mesh=mesh,
        in_specs=placed,
        out_specs=(P("dp", None), P("dp", None), P("dp", None), P(None, ("dp", "tensor")), P("dp")),
        check_vma=False,
    )
```

profile of v0, /device:TPU:1, one launch (start us, length us, event | category | flops | bytes accessed | tf_op | source)
XLA Modules:
  0.0 542.9 jit_solution(14106303053392178576)
XLA Ops:
  14.3 7.6 %scatter_custom_fusion = s32[256]{0:T(256)S(1)} fusion(s32[1024]{0:T(1024)S(1)} %bitcast.34, s32[1024]{0:T(1024)S(1)} %broadcast.354, s32[]{:T(128)} %constant.98.clone.1), kind=kCustom, calls=%fused_computation.108 | custom fusion | flops 1024 | bytes 1028 | tf_op jit(solution)/shard_map/scatter-add | solution.py:139
  28.3 98.2 %all-gather.8.cloned.1.call-done = bf16[512,16384]{1,0:T(8,128)(2,1)} async-done(((bf16[512,1024]{1,0:T(8,128)(2,1)}), bf16[512,16384]{1,0:T(8,128)(2,1)}) %all-gather.8.cloned.1.call-update) | async-done | bytes 16777232 | tf_op jit(solution)/shard_map/all_gather | solution.py:18
  126.5 10.3 %multiply_reduce_fusion.5 = (f32[16384]{0:T(1024)S(1)}, f32[256,16384]{1,0:T(8,128)}) fusion(f32[256]{0:T(256)S(1)} %get-tuple-element.27, bf16[512,16384]{1,0:T(8,128)(2,1)} %all-gather.8.cloned.1.call-done, f32[256]{0:T(256)S(1)} %add_rsqrt_fusion, bf16[256,256]{1,0:T(8,128)(2,1)S(1)} %gather_fusion.1, pred[256]{0:T(512)(128)(4,1)S(1)} %get-tuple-element.28), kind=kOutput, calls=%fused_computation.15 | convolution fusion | flops 2164506624 | bytes 25364736 | tf_op jit(solution)/shard_map/dot_general | solution.py:92
  137.7 24.9 %all_to_all.53 = f32[16,1,16384]{2,1,0:T(1,128)} all-to-all(f32[16,1,16384]{2,1,0:T(1,128)S(1)} %broadcast_in_dim.94), channel_id=1, replica_groups=mesh['dp'=16,'tensor'=8] {'dp'}, dimensions={0} | all-to-all | bytes 2097152 | tf_op jit(solution)/shard_map/all_to_all | solution.py:27
  164.5 7.8 %multiply_reduce_fusion.4 = f32[256]{0:T(256)S(1)} fusion(f32[256,16384]{1,0:T(8,128)} %get-tuple-element.23, f32[16384]{0:T(1024)S(1)} %broadcast_divide_fusion.2), kind=kLoop, calls=%fused_computation.14 | loop fusion | flops 8388352 | bytes 16843776 | tf_op jit(solution)/shard_map/reduce_sum | solution.py:101
  172.3 10.5 %all_to_all.54 = f32[8,1,256]{2,1,0:T(1,128)S(1)} all-to-all(f32[8,1,256]{2,1,0:T(1,128)S(1)} %broadcast_in_dim.95), channel_id=1, replica_groups=mesh['dp'=16,'tensor'=8] {'tensor'}, dimensions={0} | all-to-all | bytes 16384 | tf_op jit(solution)/shard_map/all_to_all | solution.py:27
  183.5 8.0 %multiply_reduce_fusion.3 = f32[16384]{0:T(1024)S(1)} fusion(f32[256,16384]{1,0:T(8,128)} %get-tuple-element.23, f32[256]{0:T(256)S(1)} %subtract_divide_fusion.3), kind=kLoop, calls=%fused_computation.13 | loop fusion | flops 8372224 | bytes 16843776 | tf_op jit(solution)/shard_map/reduce_sum | solution.py:98
  193.3 4.3 all-to-all-start.3
  198.4 15.7 %all-to-all-done.3 = f32[16,1,16384]{2,1,0:T(1,128)} async-done(((f32[16,1,16384]{2,1,0:T(1,128)}), f32[16,1,16384]{2,1,0:T(1,128)}, u32[]{:S(2)}, u32[]{:S(2)}) %all-to-all-start.3) | async-done | bytes 1048608 | tf_op jit(solution)/shard_map/all_to_all | solution.py:27
  216.0 7.5 %multiply_reduce_fusion.2 = f32[256]{0:T(256)S(1)} fusion(f32[256,16384]{1,0:T(8,128)} %get-tuple-element.23, f32[16384]{0:T(1024)S(1)} %broadcast_divide_fusion.1), kind=kLoop, calls=%fused_computation.12 | loop fusion | flops 8388352 | bytes 16843776 | tf_op jit(solution)/shard_map/reduce_sum | solution.py:101
  224.1 5.2 all-to-all-start.4
  234.8 7.8 %multiply_reduce_fusion.1 = f32[16384]{0:T(1024)S(1)} fusion(f32[256,16384]{1,0:T(8,128)} %get-tuple-element.23, f32[256]{0:T(256)S(1)} %subtract_divide_fusion.2), kind=kLoop, calls=%fused_computation.11 | loop fusion | flops 8372224 | bytes 16843776 | tf_op jit(solution)/shard_map/reduce_sum | solution.py:98
  248.1 6.1 %multiply_convert_fusion.1 = (bf16[256,2048]{1,0:T(8,128)(2,1)S(1)}, f32[256,2048]{1,0:T(8,128)}) fusion(bf16[1536,2048]{1,0:T(8,128)(2,1)} %all-gather.4.cloned.1.call-done, bf16[256,1536]{1,0:T(8,128)(2,1)S(1)} %copy-done.3, pred[256]{0:T(512)(128)(4,1)S(1)} %get-tuple-element.28), kind=kOutput, calls=%fused_computation.36 | convolution fusion | flops 1613627392 | bytes 10223872 | tf_op jit(solution)/shard_map/dot_general | solution.py:72
  256.3 8.1 %all-to-all-done.5 = f32[16,1,16384]{2,1,0:T(1,128)S(1)} async-done(((f32[16,1,16384]{2,1,0:T(1,128)}), f32[16,1,16384]{2,1,0:T(1,128)S(1)}, u32[]{:S(2)}, u32[]{:S(2)}) %all-to-all-start.5) | async-done | bytes 1048608 | tf_op jit(solution)/shard_map/all_to_all | solution.py:27
  265.1 16.1 %multiply_reduce_fusion = (f32[256]{0:T(256)S(1)}, f32[256]{0:T(256)S(1)}, f32[256]{0:T(256)S(1)}, f32[256,16384]{1,0:T(8,128)}) fusion(f32[256,16384]{1,0:T(8,128)} %get-tuple-element.23, f32[16384]{0:T(1024)S(1)} %broadcast_divide_fusion, bf16[512,16384]{1,0:T(8,128)(2,1)} %all-gather.8.cloned.1.call-done, f32[256,256]{0,1:T(8,128)S(1)} %get-tuple-element.21, ...), kind=kOutput, calls=%fused_computation.9 | convolution fusion | flops 2172779776 | bytes 42274816 | tf_op jit(solution)/shard_map/dot_general | solution.py:94
  281.2 9.0 %all_to_all.55 = f32[8,1,256]{2,1,0:T(1,128)S(1)} all-to-all(f32[8,1,256]{2,1,0:T(1,128)S(1)} %broadcast_in_dim.91), channel_id=1, replica_groups=mesh['dp'=16,'tensor'=8] {'tensor'}, dimensions={0} | all-to-all | bytes 16384 | tf_op jit(solution)/shard_map/all_to_all | solution.py:27
  290.3 7.7 %all_to_all.56 = f32[8,1,256]{2,1,0:T(1,128)S(1)} all-to-all(f32[8,1,256]{2,1,0:T(1,128)S(1)} %broadcast_in_dim.99), channel_id=1, replica_groups=mesh['dp'=16,'tensor'=8] {'tensor'}, dimensions={0} | all-to-all | bytes 16384 | tf_op jit(solution)/shard_map/all_to_all | solution.py:27
  302.5 4.6 all-to-all-done.8
  308.0 12.1 %multiply_convert_fusion = bf16[256,16384]{1,0:T(8,128)(2,1)S(1)} fusion(f32[256,16384]{1,0:T(8,128)} %get-tuple-element.24, f32[256,16384]{1,0:T(8,128)} %get-tuple-element.23, f32[256]{0:T(256)S(1)} %get-tuple-element.17, f32[16384]{0:T(1024)S(1)} %broadcast_divide_fusion, f32[256]{0:T(256)S(1)} %reduce_sum.260, f32[256]{0:T(256)S(1)} %fusion.26), kind=kLoop, calls=%fused_computation.10 | loop fusion | flops 29360128 | bytes 42011648 | tf_op jit(solution)/shard_map/convert_element_type | solution.py:110
  320.1 8.8 %fusion.3 = f32[256,256]{1,0:T(8,128)S(1)} fusion(bf16[256,16384]{1,0:T(8,128)(2,1)S(1)} %multiply_convert_fusion, bf16[512,16384]{1,0:T(8,128)(2,1)} %all-gather.8.cloned.1.call-done), kind=kOutput, calls=%fused_computation.22 | convolution fusion | flops 2147483648 | bytes 17039360 | tf_op jit(solution)/shard_map/dot_general | solution.py:111
  330.4 4.2 all-to-all-start.7
  334.8 9.0 %convolution_convert_fusion = bf16[256,16384]{1,0:T(8,128)(2,1)} fusion(bf16[256,16384]{1,0:T(8,128)(2,1)} %copy-done.2, f32[256,256]{0,1:T(8,128)S(1)} %get-tuple-element.21, f32[256]{0:T(256)S(1)} %add_rsqrt_fusion.1), kind=kOutput, calls=%fused_computation.8 | convolution fusion | flops 2151809024 | bytes 17040384 | tf_op jit(solution)/shard_map/dot_general | solution.py:182
  343.8 8.0 %copy.38 = bf16[32,16,8,1024]{3,2,0,1:T(8,128)(2,1)} copy(bf16[32,16,8,1024]{3,2,1,0:T(8,128)(2,1)} %bitcast.27) | data formatting | bytes 16777216 | tf_op jit(solution)/shard_map/reshape | solution.py:36
  351.8 11.3 %copy.36 = bf16[2,8,256,1024]{3,1,2,0:T(8,128)(2,1)} copy(bf16[2,8,256,1024]{3,2,1,0:T(8,128)(2,1)} %bitcast.28) | data formatting | bytes 16777216
  368.9 4.5 convolution_convert_fusion.1
  373.4 6.5 %reshape_reshape.6 = bf16[16,196608]{1,0:T(8,128)(2,1)} reshape(bf16[1536,2048]{1,0:T(8,128)(2,1)} %convolution_convert_fusion.1) | data formatting | bytes 12582912 | tf_op jit(solution)/shard_map/reshape;reshape | solution.py:43
  379.8 19.4 %pad_maximum_fusion = bf16[16,491520]{1,0:T(8,128)(2,1)} fusion(bf16[16,262144]{1,0:T(8,128)(2,1)} %bitcast.29, bf16[16,32768]{1,0:T(8,128)(2,1)S(1)} %reshape_reshape.7, bf16[16,196608]{1,0:T(8,128)(2,1)} %reshape_reshape.6), kind=kLoop, calls=%fused_computation.17 | loop fusion | flops 47185920 | bytes 31457280 | tf_op jit(solution)/shard_map/concatenate | solution.py:43
  399.3 20.0 %reshape.334 = bf16[61440,128]{1,0:T(8,128)(2,1)} reshape(bf16[16,491520]{1,0:T(8,128)(2,1)} %pad_maximum_fusion) | data formatting | bytes 31457280 | tf_op jit(solution)/shard_map/reshape | solution.py:45
  419.8 5.8 %convolution_multiply_fusion.2 = f32[256,1536]{1,0:T(8,128)} fusion(bf16[256,2048]{1,0:T(8,128)(2,1)S(1)} %fusion.8, bf16[1536,2048]{1,0:T(8,128)(2,1)} %all-gather.4.cloned.1.call-done, f32[256]{0:T(256)S(1)} %get-tuple-element.27), kind=kOutput, calls=%fused_computation.28 | convolution fusion | flops 1611005952 | bytes 8913920 | tf_op jit(solution)/shard_map/dot_general | solution.py:130
  425.6 7.7 %scatter_custom_fusion.1 = f32[1024,1536]{1,0:T(8,128)} fusion(s32[256]{0:T(256)S(1)} %bitcast.32, f32[256,1536]{1,0:T(8,128)} %convolution_multiply_fusion.2, f32[]{:T(128)} %constant.97.clone.1), kind=kCustom, calls=%fused_computation.26 | custom fusion | flops 393216 | bytes 6291968 | tf_op jit(solution)/shard_map/scatter-add | solution.py:207
  433.3 4.9 convert_element_type.134
  438.3 83.5 %reduce-scatter.2.cloned.1.call-done = bf16[3840,128]{1,0:T(8,128)(2,1)} async-done(((bf16[61440,128]{1,0:T(8,128)(2,1)}), bf16[3840,128]{1,0:T(8,128)(2,1)}) %reduce-scatter.2.cloned.1.call-update) | async-done | bytes 983056 | tf_op jit(solution)/shard_map/reduce_scatter | solution.py:46
  (96 shorter events, 63.3 us)
Async XLA Ops:
  7.2 222.2 %copy-start = (bf16[1024,1536]{1,0:T(8,128)(2,1)S(1)}, bf16[1024,1536]{1,0:T(8,128)(2,1)}, u32[]{:S(2)}) copy-start(bf16[1024,1536]{1,0:T(8,128)(2,1)} %param.7) | copy-start | bytes 9437188
  7.2 119.4 %all-gather.8.cloned.1.call-start = ((), (), s32[]{:S(2)}) async-start(), calls=%async_computation.12 | async-start | bytes 17825792 | tf_op jit(solution)/shard_map/all_gather | solution.py:18
  12.3 235.8 %all-gather.4.cloned.1.call-start = ((), (), s32[]{:S(2)}) async-start(), calls=%async_computation.10 | async-start | bytes 6684672 | tf_op jit(solution)/shard_map/all_gather | solution.py:153
  193.3 20.8 %all-to-all-start.3 = ((f32[16,1,16384]{2,1,0:T(1,128)}), f32[16,1,16384]{2,1,0:T(1,128)}, u32[]{:S(2)}, u32[]{:S(2)}) async-start(f32[16,1,16384]{2,1,0:T(1,128)} %broadcast_in_dim.96), calls=%async_computation.3 | async-start | bytes 2097152 | tf_op jit(solution)/shard_map/all_to_all | solution.py:27
  197.6 56.5 %all-gather.6.cloned.1.call-start = ((), (), s32[]{:S(2)}) async-start(), calls=%async_computation.11 | async-start | bytes 1114112 | tf_op jit(solution)/shard_map/all_gather | solution.py:154
  224.1 9.9 %all-to-all-start.4 = ((f32[8,1,256]{2,1,0:T(1,128)}), f32[8,1,256]{2,1,0:T(1,128)S(1)}, u32[]{:S(2)}, u32[]{:S(2)}) async-start(f32[8,1,256]{2,1,0:T(1,128)} %broadcast_in_dim.97), calls=%async_computation.4 | async-start | bytes 16384 | tf_op jit(solution)/shard_map/all_to_all | solution.py:27
  234.8 13.3 %copy-start.3 = (bf16[256,1536]{1,0:T(8,128)(2,1)S(1)}, bf16[256,1536]{1,0:T(8,128)(2,1)}, u32[]{:S(2)}) copy-start(bf16[256,1536]{1,0:T(8,128)(2,1)} %gather_fusion) | copy-start | bytes 2359300
  244.4 20.0 %all-to-all-start.5 = ((f32[16,1,16384]{2,1,0:T(1,128)}), f32[16,1,16384]{2,1,0:T(1,128)S(1)}, u32[]{:S(2)}, u32[]{:S(2)}) async-start(f32[16,1,16384]{2,1,0:T(1,128)} %broadcast_in_dim.98), calls=%async_computation.5 | async-start | bytes 2097152 | tf_op jit(solution)/shard_map/all_to_all | solution.py:27
  254.2 27.1 %copy-start.4 = (bf16[256,2048]{1,0:T(8,128)(2,1)}, bf16[256,2048]{1,0:T(8,128)(2,1)S(1)}, u32[]{:S(2)}) copy-start(bf16[256,2048]{1,0:T(8,128)(2,1)S(1)} %get-tuple-element.18) | copy-start | bytes 3145732
  298.5 8.6 %all-to-all-start.8 = ((f32[8,1,256]{2,1,0:T(1,128)}), f32[8,1,256]{2,1,0:T(1,128)S(1)}, u32[]{:S(2)}, u32[]{:S(2)}) async-start(f32[8,1,256]{2,1,0:T(1,128)} %broadcast_in_dim.101), calls=%async_computation.9 | async-start | bytes 16384 | tf_op jit(solution)/shard_map/all_to_all | solution.py:27
  320.1 8.8 %copy-start.2 = (bf16[256,16384]{1,0:T(8,128)(2,1)}, bf16[256,16384]{1,0:T(8,128)(2,1)S(1)}, u32[]{:S(2)}) copy-start(bf16[256,16384]{1,0:T(8,128)(2,1)S(1)} %multiply_convert_fusion) | copy-start | bytes 25165828
  330.4 32.7 %all-to-all-start.7 = ((f32[8,256,256]{2,1,0:T(8,128)}), f32[8,256,256]{2,1,0:T(8,128)S(1)}, u32[]{:S(2)}, u32[]{:S(2)}) async-start(f32[8,256,256]{2,1,0:T(8,128)} %broadcast_in_dim.100), calls=%async_computation.7 | async-start | bytes 4194304 | tf_op jit(solution)/shard_map/all_to_all | solution.py:27
  334.6 187.1 %reduce-scatter.2.cloned.1.call-start = ((), (), s32[]{:S(2)}) async-start(), calls=%async_computation.13 | async-start | bytes 16711680 | tf_op jit(solution)/shard_map/reduce_scatter | solution.py:46
  425.6 110.3 %copy-start.1 = (bf16[1024,1536]{1,0:T(8,128)(2,1)S(1)}, bf16[1024,1536]{1,0:T(8,128)(2,1)}, u32[]{:S(2)}) copy-start(bf16[1024,1536]{1,0:T(8,128)(2,1)} %param.7) | copy-start | bytes 9437188
Sparse Core Ops, SparseCore 0:
  12.4 114.0 all-gather.7
  128.7 69.4 all-gather.3
  200.6 40.1 all-gather.5
  419.4 102.2 reduce-scatter.1
where the time goes:
time: 553 us; the launch traced here: 543 us
  waiting for transfers between devices  214 us (39%)
  other arithmetic  110 us (20%)
  matrix products  67.2 us (12%)
  local copies, waits for them, and re-layouts  63.8 us (12%)
  blocking collectives  52 us (9%)
  starting transfers between devices  21.9 us (4%)
  between operations  14.5 us (3%)
    all_gather x1, waiting for transfers between devices, side_by_side(): filled, at, outs = (lax.all_gather(both, axis, axis=dim, tiled=True), 0, [])  98.2 us
    reduce_scatter x1, waiting for transfers between devices, sum_packed(): lax.psum_scatter(lines, axis, tiled=True).reshape(-1)  83.5 us
    all_to_all x4, blocking collectives, sent_to_all(): return lax.all_to_all(copies, axis, split_axis=0, concat_axis=0, tiled=True)  52 us
    all_to_all x5, waiting for transfers between devices, sent_to_all(): return lax.all_to_all(copies, axis, split_axis=0, concat_axis=0, tiled=True)  31 us
    all_to_all x5, starting transfers between devices, sent_to_all(): return lax.all_to_all(copies, axis, split_axis=0, concat_axis=0, tiled=True)  21.3 us
    reshape x1, local copies, waits for them, and re-layouts, sum_packed(): jnp.pad(lines, ((0, 0), (0, width * 128 - lines.shape[1]))).reshape(-1, 128)  20 us
    concatenate x1, other arithmetic, sum_packed(): lines = jnp.concatenate([b.reshape(peers, -1) for b in pieces], axis=1)  19.4 us
    dot_general x1, matrix products, prototype_terms(): jnp.dot(student_rows, student_cols, preferred_element_type=jnp.float32)  16.1 us
  transfers between devices with their start and end apart: 9, of which 6 were waited for; matrix products, arithmetic and copies ran while one was open for 23% of the time, Pallas kernels for 0%

commit v1 on v0

v1 whole, which is shorter than its diff:
```python
import jax
import jax.numpy as jnp
from jax import lax
from jax.experimental import pallas as pl
from jax.experimental.pallas import tpu as pltpu
from jax.sharding import PartitionSpec as P

ROUNDS = 3
CAP = 256
TEACHER_TEMP = 0.07
STUDENT_TEMP = 0.1
EPS = 1e-06
GRAD_SCALE = 65536.0
INTERPRET = False
f32, bf16 = (jnp.float32, jnp.bfloat16)
VMEM = pl.BlockSpec(memory_space=pltpu.VMEM)
HBM = pl.BlockSpec(memory_space=pl.ANY)
SMEM = pl.BlockSpec(memory_space=pltpu.SMEM)
NT = (((1,), (1,)), ((), ()))
TN = (((0,), (0,)), ((), ()))
EXTRA = 16


def mm(a, b, dims=None):
    if dims is None:
        return jnp.dot(a, b, preferred_element_type=f32)
    return lax.dot_general(a, b, dims, preferred_element_type=f32)


def call(body, outs, ins, out_specs=None, in_specs=None, scratch=(), name=None):
    outs = tuple(jax.ShapeDtypeStruct(s, d) for s, d in outs)
    return pl.pallas_call(
        body,
        out_shape=outs,
        in_specs=in_specs or [VMEM] * len(ins),
        out_specs=tuple(out_specs or [VMEM] * len(outs)),
        scratch_shapes=list(scratch),
        interpret=INTERPRET,
        name=name,
        compiler_params=pltpu.CompilerParams(vmem_limit_bytes=48 << 20),
    )(*ins)


def iota(shape, dim):
    return lax.broadcasted_iota(jnp.int32, shape, dim)


def select_body(mask_ref, feats_ref, sel_ref, pack_ref, member_ref):
    crops, patches = mask_ref.shape
    mask = mask_ref[...].astype(f32)
    upto = (iota((patches, patches), 0) <= iota((patches, patches), 1)).astype(f32).astype(bf16)
    rank = mm(mask.astype(bf16), upto)
    count = jnp.sum(mask, axis=1, keepdims=True)
    total = jnp.sum(count, axis=0, keepdims=True)
    slot = iota((CAP, patches), 0).astype(f32)
    lane = iota((1, CAP), 1).astype(f32)
    start = jnp.zeros((1, 1), f32)
    weight = jnp.zeros((1, CAP), f32)
    first = iota((CAP, patches), 1) == 0
    member_ref[...] = jnp.zeros_like(member_ref)
    for c in range(crops):
        hit = jnp.where((rank[c : c + 1] + start == slot + 1.0) & (mask[c : c + 1] > 0.0), 1.0, 0.0)
        if c == 0:
            hit = jnp.where(first & (slot >= total), 1.0, hit)
        sel_ref[:, c * patches : (c + 1) * patches] = hit.astype(bf16)
        own = count[c : c + 1]
        inside = jnp.where((lane >= start) & (lane < start + own), 1.0, 0.0)
        part = inside * (1.0 / jnp.maximum(own, 1.0))
        member_ref[c : c + 1, :] = part
        weight = weight + part
        start = start + own
    live = jnp.where(lane < total, 1.0, 0.0)
    picked = mm(sel_ref[...], feats_ref[...])
    scale = lax.rsqrt(jnp.sum(picked * picked, axis=1, keepdims=True) + EPS)
    pack_ref[0:CAP, :] = (picked * scale).astype(bf16)
    at = iota((EXTRA, CAP), 0)
    tail = jnp.where(at == 0, live, jnp.where(at == 1, weight * GRAD_SCALE, 0.0))
    pack_ref[CAP : CAP + EXTRA, :] = tail.astype(bf16)


def columns_body(student_ref, teacher_ref, cols_ref, student_t_ref, teacher_t_ref, norm_ref):
    width = student_ref.shape[1]
    step = min(256, width)
    for at in range(0, width, step):
        part = slice(at, at + step)
        wide = student_ref[:, part].astype(f32)
        norm = jnp.sqrt(jnp.sum(wide * wide, axis=0, keepdims=True) + EPS)
        norm_ref[:, part] = norm
        unit = wide / norm
        cols_ref[:, part] = unit.astype(bf16)
        student_t_ref[part, :] = unit.T.astype(bf16)
        wide = teacher_ref[:, part].astype(f32)
        norm = jnp.sqrt(jnp.sum(wide * wide, axis=0, keepdims=True) + EPS)
        teacher_t_ref[part, :] = (wide / norm).T.astype(bf16)


def weights_body(at_ref, w_in_ref, w_out_ref, pack_ref):
    rows, hid = w_in_ref.shape
    per = w_out_ref.shape[0]
    own = at_ref[0]
    chunk = per * 8
    row = iota((chunk, per), 0)
    col = iota((chunk, per), 1)
    pick = (row == (col // 16) * per + own * 16 + col % 16).astype(f32).astype(bf16)
    for m in range(hid // chunk):
        part = mm(w_in_ref[:, m * chunk : (m + 1) * chunk], pick)
        pack_ref[0:rows, m * per : (m + 1) * per] = part.astype(bf16)
    pack_ref[rows : rows + 16, :] = w_out_ref[pl.ds(pl.multiple_of(own * 16, 16), 16), :]


def forward_body(sel_ref, tokens_ref, pack_ref, rows_ref, hidden_ref, slope_ref, feats_ref, w_in_ref, w_out_ref):
    peers, lines, width = pack_ref.shape
    per = lines - 16
    for g in range(peers):
        w_in_ref[g * per : (g + 1) * per, :] = pack_ref[g, 0:per, :]
        w_out_ref[g * 16 : (g + 1) * 16, :] = pack_ref[g, per:lines, :]
    rows = mm(sel_ref[...], tokens_ref[...]).astype(bf16)
    rows_ref[...] = rows
    pre = mm(rows, w_in_ref[...])
    cdf = 0.5 * (1.0 + lax.erf(pre * 0.7071067811865476))
    slope_ref[...] = cdf + pre * (jnp.exp(-0.5 * pre * pre) * 0.3989422804014327)
    hidden = (pre * cdf).astype(bf16)
    hidden_ref[...] = hidden
    feats_ref[...] = mm(hidden, w_out_ref[...])


def unit_body(feats_ref, unit_ref, inv_ref, rows_ref):
    feats = feats_ref[...]
    inv = lax.rsqrt(jnp.sum(feats * feats, axis=1, keepdims=True) + EPS)
    unit = feats * inv
    unit_ref[...] = unit.T
    inv_ref[...] = jnp.broadcast_to(inv, feats.shape).T[0:8]
    rows_ref[...] = unit.astype(bf16)


def chunks_of(width):
    step = min(256, width)
    return [slice(at, at + step) for at in range(0, width, step)]


def row_of(ref, g):
    return ref[pl.ds(g, 1), :]


def fold(x):
    return x.reshape(x.shape[0] // 8, 8, x.shape[1]).sum(axis=0)


def expo_body(cols_ref, pack_ref, expo_hbm, part_ref, live_ref, weight_ref, expo_ref, total_ref, sems):
    peers = pack_ref.shape[0]
    width = cols_ref.shape[0]
    total_ref[...] = jnp.zeros_like(total_ref)

    def first(g, _):
        rows = pack_ref[g, 0:CAP, :]
        tail = pack_ref[g, CAP : CAP + EXTRA, :].astype(f32)
        live = tail[0:1]
        live_ref[pl.ds(g, 1), :] = live
        weight_ref[pl.ds(g, 1), :] = tail[1:2]
        for part in chunks_of(width):
            cos = mm(cols_ref[part, :], rows, NT)
            expo = jnp.exp(cos * (1.0 / TEACHER_TEMP)) * live
            expo_ref[g, part, :] = expo.astype(bf16)
            total_ref[part, :] += expo[:, 0:128] + expo[:, 128:256]
        pltpu.make_async_copy(expo_ref.at[g], expo_hbm.at[g], sems.at[g]).start()
        return 0

    lax.fori_loop(0, peers, first, 0)
    spread_scale(total_ref)
    lax.fori_loop(0, peers, lambda g, _: row_part(g, expo_ref, total_ref, part_ref), 0)

    def last(g, _):
        pltpu.make_async_copy(expo_ref.at[g], expo_hbm.at[g], sems.at[g]).wait()
        return 0

    lax.fori_loop(0, peers, last, 0)


def spread_scale(total_ref):
    for part in chunks_of(total_ref.shape[0]):
        sums = jnp.sum(total_ref[part, :], axis=1, keepdims=True)
        total_ref[part, :] = jnp.broadcast_to(1.0 / sums, sums.shape[:1] + (128,))


def scaled(expo, scale):
    return jnp.concatenate([expo[:, 0:128] * scale, expo[:, 128:256] * scale], axis=1)


def row_part(g, expo_ref, scale_ref, part_ref):
    acc = jnp.zeros((8, CAP), f32)
    for part in chunks_of(scale_ref.shape[0]):
        acc = acc + fold(scaled(expo_ref[g, part, :].astype(f32), scale_ref[part, :]))
    part_ref[pl.ds(g, 1), :] = jnp.sum(acc, axis=0, keepdims=True)
    return 0


def load_expo(expo_hbm, expo_ref, sems, peers):
    def begin(g, _):
        pltpu.make_async_copy(expo_hbm.at[g], expo_ref.at[g], sems.at[g]).start()
        return 0

    lax.fori_loop(0, peers, begin, 0)


def column_sums(expo_hbm, expo_ref, sems, scale, total_ref, peers):
    def step(g, _):
        pltpu.make_async_copy(expo_hbm.at[g], expo_ref.at[g], sems.at[g]).wait()
        row = row_of(scale, g)
        for part in chunks_of(total_ref.shape[0]):
            expo = expo_ref[g, part, :].astype(f32)
            total_ref[part, :] += expo[:, 0:128] * row[:, 0:128] + expo[:, 128:256] * row[:, 128:256]
        return 0

    lax.fori_loop(0, peers, step, 0)


def balance_body(expo_hbm, sums_ref, live_ref, part_ref, expo_ref, total_ref, scale_ref, sems):
    peers = live_ref.shape[0]
    load_expo(expo_hbm, expo_ref, sems, peers)
    live = live_ref[...]
    scale_ref[...] = live / (sums_ref[...] + 1.0 - live)
    total_ref[...] = jnp.zeros_like(total_ref)
    column_sums(expo_hbm, expo_ref, sems, scale_ref, total_ref, peers)
    spread_scale(total_ref)
    lax.fori_loop(0, peers, lambda g, _: row_part(g, expo_ref, total_ref, part_ref), 0)


def last_body(expo_hbm, sums_ref, live_ref, cols_ref, part_ref, pull_ref, total_ref, expo_ref, scale_ref, sems):
    peers = live_ref.shape[0]
    load_expo(expo_hbm, expo_ref, sems, peers)
    live = live_ref[...]
    scale_ref[...] = live / (sums_ref[...] + 1.0 - live)
    total_ref[...] = jnp.zeros_like(total_ref)
    column_sums(expo_hbm, expo_ref, sems, scale_ref, total_ref, peers)
    spread_scale(total_ref)

    def step(g, _):
        acc = jnp.zeros((8, CAP), f32)
        pull = jnp.zeros((cols_ref.shape[0], CAP), f32)
        for part in chunks_of(total_ref.shape[0]):
            balanced = scaled(expo_ref[g, part, :].astype(f32), total_ref[part, :])
            acc = acc + fold(balanced)
            pull = pull + mm(cols_ref[:, part], balanced.astype(bf16))
        part_ref[pl.ds(g, 1), :] = jnp.sum(acc, axis=0, keepdims=True)
        pull_ref[g] = pull.astype(bf16)
        return 0

    lax.fori_loop(0, peers, step, 0)


def student_body(cols_t_ref, cols_ref, rows_ref, raised_hbm, part_ref, pull_ref, raised_ref, sems):
    peers = rows_ref.shape[0]
    width = cols_t_ref.shape[0]

    def step(g, _):
        rows = rows_ref[g]
        acc = jnp.zeros((8, CAP), f32)
        pull = jnp.zeros((cols_ref.shape[0], CAP), f32)
        for part in chunks_of(width):
            raised = jnp.exp(mm(cols_t_ref[part, :], rows, NT) * (1.0 / STUDENT_TEMP))
            acc = acc + fold(raised)
            raised = raised.astype(bf16)
            raised_ref[g, part, :] = raised
            pull = pull + mm(cols_ref[:, part], raised)
        part_ref[pl.ds(g, 1), :] = jnp.sum(acc, axis=0, keepdims=True)
        pull_ref[g] = pull.astype(bf16)
        pltpu.make_async_copy(raised_ref.at[g], raised_hbm.at[g], sems.at[g]).start()
        return 0

    lax.fori_loop(0, peers, step, 0)

    def last(g, _):
        pltpu.make_async_copy(raised_ref.at[g], raised_hbm.at[g], sems.at[g]).wait()
        return 0

    lax.fori_loop(0, peers, last, 0)


def columns_grad_body(
    expo_hbm, raised_hbm, scale_ref, norm_sum_ref, sums_ref, live_ref, weight_ref, rows_ref, proto_ref, norm_ref,
    grad_ref, expo_ref, raised_ref, acc_ref, alpha_ref, beta_ref, esems, rsems,
):
    peers = live_ref.shape[0]
    load_expo(expo_hbm, expo_ref, esems, peers)
    load_expo(raised_hbm, raised_ref, rsems, peers)
    live = live_ref[...]
    weight = weight_ref[...] * (1.0 / STUDENT_TEMP)
    alpha_ref[...] = weight / norm_sum_ref[...]
    beta_ref[...] = weight * (live / (sums_ref[...] + 1.0 - live))
    acc_ref[...] = jnp.zeros_like(acc_ref)

    def step(g, _):
        pltpu.make_async_copy(expo_hbm.at[g], expo_ref.at[g], esems.at[g]).wait()
        pltpu.make_async_copy(raised_hbm.at[g], raised_ref.at[g], rsems.at[g]).wait()
        alpha, beta = (row_of(alpha_ref, g), row_of(beta_ref, g))
        rows = rows_ref[g]
        for part in chunks_of(acc_ref.shape[0]):
            balanced = scaled(expo_ref[g, part, :].astype(f32), scale_ref[part, :])
            score = raised_ref[g, part, :].astype(f32) * alpha - balanced * beta
            acc_ref[part, :] += mm(score.astype(bf16), rows)
        return 0

    lax.fori_loop(0, peers, step, 0)
    for part in chunks_of(acc_ref.shape[0]):
        grad = acc_ref[part, :].T
        norm = norm_ref[:, part]
        unit = proto_ref[:, part].astype(f32) / norm
        grad_ref[:, part] = (grad - unit * jnp.sum(unit * grad, axis=0, keepdims=True)) / norm


def backward_body(
    push_ref, pull_ref, norm_sum_ref, sums_ref, pack_ref, member_ref, unit_ref, inv_ref, rows_ref, hidden_ref, slope_ref,
    w_ref, send_ref, grad_rows_ref, loss_ref, w_in_ref, w_out_ref,
):
    peers, lines, width = w_ref.shape
    per = lines - 16
    for g in range(peers):
        w_in_ref[g * per : (g + 1) * per, :] = w_ref[g, 0:per, :]
        w_out_ref[g * 16 : (g + 1) * 16, :] = w_ref[g, per:lines, :]
    tail = pack_ref[CAP : CAP + EXTRA, :].astype(f32)
    live, weight = (tail[0:1], tail[1:2])
    norm_sum = norm_sum_ref[...]
    scale = live / (sums_ref[...] + 1.0 - live)
    pull = pull_ref[...]
    unit = unit_ref[...]
    cross = jnp.sum(unit.astype(bf16).astype(f32) * pull, axis=0, keepdims=True) * (1.0 / STUDENT_TEMP)
    row_loss = jnp.log(norm_sum) - scale * cross
    loss = jnp.sum(member_ref[...] * row_loss, axis=1, keepdims=True)
    loss_ref[...] = jnp.broadcast_to(loss, loss_ref.shape)
    grad_unit = (weight * (1.0 / STUDENT_TEMP)) * (push_ref[...] / norm_sum - scale * pull)
    inner = jnp.sum(unit * grad_unit, axis=0, keepdims=True)
    grad_feats = (inv_ref[0:1] * (grad_unit - unit * inner)).T.astype(bf16)
    hidden = hidden_ref[...]
    grad_out = mm(hidden, grad_feats, TN).astype(bf16)
    grad_pre = (mm(grad_feats, w_out_ref[...], NT) * slope_ref[...]).astype(bf16)
    grad_in = mm(rows_ref[...], grad_pre, TN).astype(bf16)
    for g in range(peers):
        send_ref[g, 0:per, :] = grad_in[g * per : (g + 1) * per, :]
        send_ref[g, per:lines, :] = grad_out[g * 16 : (g + 1) * 16, :]
    grad_rows_ref[...] = mm(grad_pre, w_in_ref[...], NT).astype(bf16)


def place_body(sel_ref, rows_ref, out_ref):
    out_ref[...] = mm(sel_ref[...], rows_ref[...], TN).astype(bf16)


def weight_grads_body(parts_ref, grad_in_ref, grad_out_ref):
    peers, lines, width = parts_ref.shape
    per = lines - 16
    wide = peers * 128
    row = iota((wide, wide), 0)
    col = iota((wide, wide), 1)
    goes = (col // 128) * 16 + ((col % 128) // 16) * 128 + col % 16
    order = (row == goes).astype(f32).astype(bf16)
    for m in range(width // 128):
        block = jnp.concatenate([parts_ref[t, 0:per, m * 128 : (m + 1) * 128] for t in range(peers)], axis=1)
        grad_in_ref[:, m * wide : (m + 1) * wide] = mm(block, order)
    for t in range(peers):
        grad_out_ref[t * 16 : (t + 1) * 16, :] = parts_ref[t, per:lines, :].astype(f32)


def exchange(x, axis):
    return lax.all_to_all(x, axis, split_axis=0, concat_axis=0, tiled=True)


def spread(x, axis):
    return exchange(jnp.broadcast_to(x, (lax.axis_size(axis), *x.shape)), axis)


def total(x):
    return x.astype(f32).sum(axis=0)


def everywhere(x):
    return total(spread(total(spread(x, "tensor")), "dp"))


def shards(tokens, teacher_feats, masks, w_in, w_out, proto_student, proto_teacher):
    dim = tokens.shape[1]
    hid = w_in.shape[1]
    bot, width = proto_student.shape
    dp, tensor = (lax.axis_size("dp"), lax.axis_size("tensor"))
    per = w_in.shape[0]
    lines = per + 16
    me = lax.axis_index("dp")
    own = lax.axis_index("tensor").astype(jnp.int32).reshape(1)
    part_hid = hid // tensor

    sel, pack, member = call(
        select_body,
        [((CAP, tokens.shape[0]), bf16), ((CAP + EXTRA, bot), bf16), ((8, CAP), f32)],
        (masks, teacher_feats),
        name="select",
    )
    packs = spread(pack, "dp")
    (w_pack,) = call(
        weights_body, [((lines, part_hid), bf16)], (own, w_in, w_out), in_specs=[SMEM, VMEM, VMEM], name="weights"
    )
    w_packs = spread(w_pack, "dp")
    cols, student_t, teacher_t, norm = call(
        columns_body,
        [((bot, width), bf16), ((width, bot), bf16), ((width, bot), bf16), ((1, width), f32)],
        (proto_student, proto_teacher),
        name="columns",
    )
    big = ((dp, width, CAP), bf16)
    small = ((dp, CAP), f32)
    held = pltpu.VMEM(*big)
    sems = pltpu.SemaphoreType.DMA((dp,))
    sums = pltpu.VMEM((width, 128), f32)
    expo, part, live, weight = call(
        expo_body,
        [big, small, small, small],
        (teacher_t, packs),
        out_specs=[HBM, VMEM, VMEM, VMEM],
        scratch=[held, sums, sems],
        name="expo",
    )
    rows, hidden, slope, feats_part = call(
        forward_body,
        [((CAP, dim), bf16), ((CAP, part_hid), bf16), ((CAP, part_hid), f32), ((CAP, bot), f32)],
        (sel, tokens, w_packs),
        scratch=[pltpu.VMEM((dim, part_hid), bf16), pltpu.VMEM((part_hid, bot), bf16)],
        name="forward",
    )
    feats = total(exchange(feats_part.reshape(tensor, CAP // tensor, bot), "tensor"))
    feats = spread(feats, "tensor").reshape(CAP, bot)
    unit, inv, student_rows = call(
        unit_body, [((bot, CAP), f32), ((8, CAP), f32), ((CAP, bot), bf16)], (feats,), name="unit"
    )
    all_rows = spread(student_rows, "dp")
    row_sum = everywhere(part)
    raised, norm_part, push = call(
        student_body,
        [big, small, ((dp, bot, CAP), bf16)],
        (student_t, cols, all_rows),
        out_specs=[HBM, VMEM, VMEM],
        scratch=[held, sems],
        name="student",
    )
    (part,) = call(
        balance_body,
        [small],
        (expo, row_sum, live),
        in_specs=[HBM, VMEM, VMEM],
        scratch=[held, sums, pltpu.VMEM(*small), sems],
        name="balance",
    )
    both = everywhere(jnp.concatenate([part, norm_part], axis=0))
    row_sum, norm_sum = (both[:dp], both[dp:])
    push_own = total(spread(total(exchange(push, "dp")).astype(bf16), "tensor"))
    part, pull, scale = call(
        last_body,
        [small, ((dp, bot, CAP), bf16), ((width, 128), f32)],
        (expo, row_sum, live, cols),
        in_specs=[HBM, VMEM, VMEM, VMEM],
        scratch=[held, pltpu.VMEM(*small), sems],
        name="last",
    )
    row_sum = everywhere(part)
    pull_own = total(spread(total(exchange(pull, "dp")).astype(bf16), "tensor"))
    (grad_proto,) = call(
        columns_grad_body,
        [((bot, width), f32)],
        (expo, raised, scale, norm_sum, row_sum, live, weight, all_rows, proto_student, norm),
        in_specs=[HBM, HBM] + [VMEM] * 8,
        scratch=[held, held, pltpu.VMEM((width, bot), f32), pltpu.VMEM(*small), pltpu.VMEM(*small), sems, sems],
        name="columns_grad",
    )
    mine = lambda x: lax.dynamic_slice_in_dim(x, me, 1, axis=0)
    send, grad_rows, loss = call(
        backward_body,
        [((dp, lines, part_hid), bf16), ((CAP, dim), bf16), ((8, 128), f32)],
        (push_own, pull_own, mine(norm_sum), mine(row_sum), pack, member, unit, inv, rows, hidden, slope, w_packs),
        scratch=[pltpu.VMEM((dim, part_hid), bf16), pltpu.VMEM((part_hid, bot), bf16)],
        name="backward",
    )
    weight_part = total(exchange(send, "dp")).astype(bf16)
    rows_part = total(exchange(grad_rows.reshape(tensor, CAP // tensor, dim), "tensor")).astype(bf16)
    weight_parts = spread(weight_part, "tensor")
    rows_full = spread(rows_part, "tensor").reshape(CAP, dim)
    grad_in, grad_out = call(
        weight_grads_body,
        [((per, hid), f32), ((w_out.shape[0], bot), f32)],
        (weight_parts,),
        name="weight_grads",
    )
    (d_tokens,) = call(place_body, [(tokens.shape, bf16)], (sel, rows_full), name="place")
    return (d_tokens, grad_in, grad_out, grad_proto, loss[: masks.shape[0], 0])


def solution(mesh):
    placed = (
        P("dp", None),
        P("dp", None),
        P("dp", None),
        P("dp", None),
        P("dp", None),
        P(None, ("dp", "tensor")),
        P(None, ("dp", "tensor")),
    )
    return jax.shard_map(
        shards,
        mesh=mesh,
        in_specs=placed,
        out_specs=(P("dp", None), P("dp", None), P("dp", None), P(None, ("dp", "tensor")), P("dp")),
        check_vma=False,
    )
```

time: 553 us -> 422 us (0.76); the launches traced: 543 us -> 420 us
  other arithmetic: 110 us -> 12.9 us
  waiting for transfers between devices: 214 us -> 142 us
  matrix products: 67.2 us -> 0 us
  Pallas kernels: 0 us -> 56.9 us
  starting transfers between devices: 21.9 us -> 71.5 us
  blocking collectives: 52 us -> 97.7 us
  local copies, waits for them, and re-layouts: 63.8 us -> 38.3 us
  between operations: 14.5 us -> 1.09 us
    all_to_all x5 -> x13, waiting for transfers between devices: 31 us -> 142 us  [exchange(): return lax.all_to_all(x, axis, split_axis=0, concat_axis=0, tiled=True)]
    all_gather x3 -> x0, waiting for transfers between devices: 98.2 us -> none  [the longest x1 98.2 us: side_by_side(): filled, at, outs = (lax.all_gather(both, axis, axis=dim, tiled=True), 0, [])]
    reduce_scatter x1 -> x0, waiting for transfers between devices: 83.5 us -> none  [sum_packed(): lax.psum_scatter(lines, axis, tiled=True).reshape(-1)]
    dot_general x10 -> x0, matrix products: 67.2 us -> none  [the longest x1 16.1 us: prototype_terms(): jnp.dot(student_rows, student_cols, preferred_element_type=jnp.float32)]
    pallas_call x0 -> x13, Pallas kernels: none -> 56.9 us  [call(): pl.pallas_call(body, out_shape=outs, in_specs=in_specs or [VMEM] * len(in...]
    all_to_all x5 -> x13, starting transfers between devices: 21.3 us -> 71.5 us  [exchange(): return lax.all_to_all(x, axis, split_axis=0, concat_axis=0, tiled=True)]
    all_to_all x4 -> x6, blocking collectives: 52 us -> 97.7 us  [exchange(): return lax.all_to_all(x, axis, split_axis=0, concat_axis=0, tiled=True)]
    reduce_sum x20 -> x13, other arithmetic: 41.7 us -> 12.9 us  [total(): return x.astype(f32).sum(axis=0)]
  transfers between devices with their start and end apart: 9 -> 13, of which waited for: 6 -> 11; matrix products, arithmetic and copies ran while one was open for 23% -> 3% of each run, Pallas kernels for 0% -> 8%
where the time goes in v1:
time: 422 us; the launch traced here: 420 us
  waiting for transfers between devices  142 us (34%)
  blocking collectives  97.7 us (23%)
  starting transfers between devices  71.5 us (17%)
  Pallas kernels  56.9 us (13%)
  local copies, waits for them, and re-layouts  38.3 us (9%)
  other arithmetic  12.9 us (3%)
    all_to_all x13, waiting for transfers between devices, exchange(): return lax.all_to_all(x, axis, split_axis=0, concat_axis=0, tiled=True)  142 us
    all_to_all x6, blocking collectives, exchange(): return lax.all_to_all(x, axis, split_axis=0, concat_axis=0, tiled=True)  97.7 us
    all_to_all x13, starting transfers between devices, exchange(): return lax.all_to_all(x, axis, split_axis=0, concat_axis=0, tiled=True)  71.5 us
    pallas_call x13, Pallas kernels, call(): pl.pallas_call(body, out_shape=outs, in_specs=in_specs or [VMEM] * len(in...  56.9 us
    unnamed x98, local copies, waits for them, and re-layouts  26.4 us
    reduce_sum x13, other arithmetic, total(): return x.astype(f32).sum(axis=0)  12.9 us
    broadcast_in_dim x14, local copies, waits for them, and re-layouts, spread(): return exchange(jnp.broadcast_to(x, (lax.axis_size(axis), *x.shape)), axis)  10.1 us
  transfers between devices with their start and end apart: 13, of which 11 were waited for; matrix products, arithmetic and copies ran while one was open for 3% of the time, Pallas kernels for 8%

profile of v1, /device:TPU:1, one launch (start us, length us, event | category | flops | bytes accessed | tf_op | source)
XLA Modules:
  0.0 420.0 jit_solution(14715771395564638251)
XLA Ops:
  3.8 7.6 %all-to-all-start = ((bf16[16,112,256]{2,1,0:T(8,128)(2,1)}), bf16[16,112,256]{2,1,0:T(8,128)(2,1)S(1)}, u32[]{:S(2)}, u32[]{:S(2)}) async-start(bf16[16,112,256]{2,1,0:T(8,128)(2,1)} %broadcast_in_dim.42), calls=%async_computation | async-start | bytes 1835008 | tf_op jit(solution)/shard_map/all_to_all | solution.py:363
  12.9 13.1 %all-to-all-done.pack_ref.w_ref = bf16[16,112,256]{2,1,0:T(8,128)(2,1)S(1)} async-done(((bf16[16,112,256]{2,1,0:T(8,128)(2,1)}), bf16[16,112,256]{2,1,0:T(8,128)(2,1)S(1)}, u32[]{:S(2)}, u32[]{:S(2)}) %all-to-all-start) | async-done | bytes 917536 | tf_op jit(solution)/shard_map/all_to_all | solution.py:363
  38.2 22.3 %all-to-all-done.6.pack_ref = bf16[16,272,256]{2,1,0:T(8,128)(2,1)S(1)} async-done(((bf16[16,272,256]{2,1,0:T(8,128)(2,1)}), bf16[16,272,256]{2,1,0:T(8,128)(2,1)S(1)}, u32[]{:S(2)}, u32[]{:S(2)}) %all-to-all-start.6) | async-done | bytes 2228256 | tf_op jit(solution)/shard_map/all_to_all | solution.py:363
  60.4 9.6 %all-to-all-start.1 = ((f32[8,32,256]{2,1,0:T(8,128)}), f32[8,32,256]{2,1,0:T(8,128)}, u32[]{:S(2)}, u32[]{:S(2)}) async-start(f32[8,32,256]{2,1,0:T(8,128)} %bitcast.1), calls=%async_computation.1 | async-start | bytes 524288 | tf_op jit(solution)/shard_map/all_to_all | solution.py:363
  74.8 8.8 %expo.1 = (bf16[16,1024,256]{2,1,0:T(8,128)(2,1)}, f32[16,256]{1,0:T(8,128)S(1)}, f32[16,256]{1,0:T(8,128)S(1)}, f32[16,256]{1,0:T(8,128)S(1)}) custom-call(bf16[1024,256]{1,0:T(8,128)(2,1)S(1)} %get-tuple-element.40.cols_ref, bf16[16,272,256]{2,1,0:T(8,128)(2,1)S(1)} %all-to-all-done.6.pack_ref), custom_call_target="tpu_custom_call" | custom-call | tf_op jit(solution)/shard_map/expo/pallas_call | solution.py:32
  84.9 4.8 %all-to-all-start.7 = ((f32[8,16,256]{2,1,0:T(8,128)}), f32[8,16,256]{2,1,0:T(8,128)S(1)}, u32[]{:S(2)}, u32[]{:S(2)}) async-start(f32[8,16,256]{2,1,0:T(8,128)} %broadcast_in_dim.47), calls=%async_computation.7 | async-start | bytes 262144 | tf_op jit(solution)/shard_map/all_to_all | solution.py:363
  90.6 4.3 %all-to-all-done.7 = f32[8,16,256]{2,1,0:T(8,128)S(1)} async-done(((f32[8,16,256]{2,1,0:T(8,128)}), f32[8,16,256]{2,1,0:T(8,128)S(1)}, u32[]{:S(2)}, u32[]{:S(2)}) %all-to-all-start.7) | async-done | bytes 131104 | tf_op jit(solution)/shard_map/all_to_all | solution.py:363
  95.6 4.2 all-to-all-start.2
  99.8 6.5 %all-to-all-done.2 = f32[8,32,256]{2,1,0:T(8,128)S(1)} async-done(((f32[8,32,256]{2,1,0:T(8,128)}), f32[8,32,256]{2,1,0:T(8,128)S(1)}, u32[]{:S(2)}, u32[]{:S(2)}) %all-to-all-start.2) | async-done | bytes 262176 | tf_op jit(solution)/shard_map/all_to_all | solution.py:363
  110.8 7.3 %all-to-all-done.8 = f32[16,16,256]{2,1,0:T(8,128)S(1)} async-done(((f32[16,16,256]{2,1,0:T(8,128)}), f32[16,16,256]{2,1,0:T(8,128)S(1)}, u32[]{:S(2)}, u32[]{:S(2)}) %all-to-all-start.8) | async-done | bytes 262176 | tf_op jit(solution)/shard_map/all_to_all | solution.py:363
  124.4 5.7 %balance.1 = f32[16,256]{1,0:T(8,128)S(1)} custom-call(bf16[16,1024,256]{2,1,0:T(8,128)(2,1)} %get-tuple-element.42.expo_hbm, f32[16,256]{1,0:T(8,128)S(1)} %reduce_sum.133.sums_ref, f32[16,256]{1,0:T(8,128)S(1)} %copy-done.28), custom_call_target="tpu_custom_call" | custom-call | tf_op jit(solution)/shard_map/balance/pallas_call | solution.py:32
  130.1 20.0 %all-to-all-done.3.rows_ref = bf16[16,256,256]{2,1,0:T(8,128)(2,1)S(1)} async-done(((bf16[16,256,256]{2,1,0:T(8,128)(2,1)}), bf16[16,256,256]{2,1,0:T(8,128)(2,1)S(1)}, u32[]{:S(2)}, u32[]{:S(2)}) %all-to-all-start.3) | async-done | bytes 2097184 | tf_op jit(solution)/shard_map/all_to_all | solution.py:363
  152.2 12.1 %student.1 = (bf16[16,1024,256]{2,1,0:T(8,128)(2,1)}, f32[16,256]{1,0:T(8,128)S(1)}, bf16[16,256,256]{2,1,0:T(8,128)(2,1)S(1)}) custom-call(bf16[1024,256]{1,0:T(8,128)(2,1)S(1)} %copy-done.21, bf16[256,1024]{1,0:T(8,128)(2,1)S(1)} %copy-done.9, bf16[16,256,256]{2,1,0:T(8,128)(2,1)S(1)} %all-to-all-done.3.rows_ref), custom_call_target="tpu_custom_call" | custom-call | tf_op jit(solution)/shard_map/student/pallas_call | solution.py:32
  165.7 14.3 %all_to_all.95 = f32[8,32,256]{2,1,0:T(8,128)} all-to-all(f32[8,32,256]{2,1,0:T(8,128)S(1)} %broadcast_in_dim.49), channel_id=1, replica_groups=mesh['dp'=16,'tensor'=8] {'tensor'}, dimensions={0} | all-to-all | bytes 524288 | tf_op jit(solution)/shard_map/all_to_all | solution.py:363
  181.0 13.8 %all_to_all.96 = f32[16,32,256]{2,1,0:T(8,128)} all-to-all(f32[16,32,256]{2,1,0:T(8,128)S(1)} %broadcast_in_dim.50), channel_id=1, replica_groups=mesh['dp'=16,'tensor'=8] {'dp'}, dimensions={0} | all-to-all | bytes 1048576 | tf_op jit(solution)/shard_map/all_to_all | solution.py:363
  197.0 9.2 %last.1 = (f32[16,256]{1,0:T(8,128)S(1)}, bf16[16,256,256]{2,1,0:T(8,128)(2,1)S(1)}, f32[1024,128]{1,0:T(8,128)S(1)}) custom-call(bf16[16,1024,256]{2,1,0:T(8,128)(2,1)} %get-tuple-element.42.expo_hbm, f32[16,256]{1,0:T(8,128)S(1)} %get-tuple-element.64.sums_ref, f32[16,256]{1,0:T(8,128)S(1)} %copy-done.28, bf16[256,1024]{1,0:T(8,128)(2,1)S(1)} %copy-done.10), custom_call_target="tpu_custom_call" | custom-call | tf_op jit(solution)/shard_map/last/pallas_call | solution.py:32
  208.3 9.6 %all_to_all.97 = f32[8,16,256]{2,1,0:T(8,128)S(1)} all-to-all(f32[8,16,256]{2,1,0:T(8,128)S(1)} %broadcast_in_dim.52), channel_id=1, replica_groups=mesh['dp'=16,'tensor'=8] {'tensor'}, dimensions={0} | all-to-all | bytes 262144 | tf_op jit(solution)/shard_map/all_to_all | solution.py:363
  218.0 11.2 %all_to_all.98 = f32[16,16,256]{2,1,0:T(8,128)} all-to-all(f32[16,16,256]{2,1,0:T(8,128)S(1)} %broadcast_in_dim.53), channel_id=1, replica_groups=mesh['dp'=16,'tensor'=8] {'dp'}, dimensions={0} | all-to-all | bytes 524288 | tf_op jit(solution)/shard_map/all_to_all | solution.py:363
  229.2 31.5 %all_to_all.99 = bf16[16,256,256]{2,1,0:T(8,128)(2,1)} all-to-all(bf16[16,256,256]{2,1,0:T(8,128)(2,1)} %copy-done.6), channel_id=1, replica_groups=mesh['dp'=16,'tensor'=8] {'dp'}, dimensions={0} | all-to-all | bytes 4194304 | tf_op jit(solution)/shard_map/all_to_all | solution.py:363
  260.7 4.4 %all-to-all-start.11 = ((bf16[16,256,256]{2,1,0:T(8,128)(2,1)}), bf16[16,256,256]{2,1,0:T(8,128)(2,1)}, u32[]{:S(2)}, u32[]{:S(2)}) async-start(bf16[16,256,256]{2,1,0:T(8,128)(2,1)} %copy-done.7), calls=%async_computation.11 | async-start | bytes 4194304 | tf_op jit(solution)/shard_map/all_to_all | solution.py:363
  267.0 24.3 %all-to-all-done.11 = bf16[16,256,256]{2,1,0:T(8,128)(2,1)} async-done(((bf16[16,256,256]{2,1,0:T(8,128)(2,1)}), bf16[16,256,256]{2,1,0:T(8,128)(2,1)}, u32[]{:S(2)}, u32[]{:S(2)}) %all-to-all-start.11) | async-done | bytes 2097184 | tf_op jit(solution)/shard_map/all_to_all | solution.py:363
  292.3 9.3 %all-to-all-start.5 = ((bf16[8,256,256]{2,1,0:T(8,128)(2,1)}), bf16[8,256,256]{2,1,0:T(8,128)(2,1)}, u32[]{:S(2)}, u32[]{:S(2)}) async-start(bf16[8,256,256]{2,1,0:T(8,128)(2,1)} %broadcast_in_dim.45), calls=%async_computation.5 | async-start | bytes 2097152 | tf_op jit(solution)/shard_map/all_to_all | solution.py:363
  303.6 13.2 %all-to-all-done.5 = bf16[8,256,256]{2,1,0:T(8,128)(2,1)} async-done(((bf16[8,256,256]{2,1,0:T(8,128)(2,1)}), bf16[8,256,256]{2,1,0:T(8,128)(2,1)}, u32[]{:S(2)}, u32[]{:S(2)}) %all-to-all-start.5) | async-done | bytes 1048608 | tf_op jit(solution)/shard_map/all_to_all | solution.py:363
  317.8 5.2 %all-to-all-start.12 = ((bf16[8,256,256]{2,1,0:T(8,128)(2,1)}), bf16[8,256,256]{2,1,0:T(8,128)(2,1)}, u32[]{:S(2)}, u32[]{:S(2)}) async-start(bf16[8,256,256]{2,1,0:T(8,128)(2,1)} %broadcast_in_dim.51), calls=%async_computation.12 | async-start | bytes 2097152 | tf_op jit(solution)/shard_map/all_to_all | solution.py:363
  327.2 11.0 %all-to-all-done.12 = bf16[8,256,256]{2,1,0:T(8,128)(2,1)} async-done(((bf16[8,256,256]{2,1,0:T(8,128)(2,1)}), bf16[8,256,256]{2,1,0:T(8,128)(2,1)}, u32[]{:S(2)}, u32[]{:S(2)}) %all-to-all-start.12) | async-done | bytes 1048608 | tf_op jit(solution)/shard_map/all_to_all | solution.py:363
  345.6 17.4 %all_to_all.100 = bf16[16,112,256]{2,1,0:T(8,128)(2,1)S(1)} all-to-all(bf16[16,112,256]{2,1,0:T(8,128)(2,1)S(1)} %get-tuple-element.55), channel_id=1, replica_groups=mesh['dp'=16,'tensor'=8] {'dp'}, dimensions={0} | all-to-all | bytes 1835008 | tf_op jit(solution)/shard_map/all_to_all | solution.py:363
  363.0 6.0 %all-to-all-start.15 = ((bf16[8,32,1536]{2,1,0:T(8,128)(2,1)}), bf16[8,32,1536]{2,1,0:T(8,128)(2,1)}, u32[]{:S(2)}, u32[]{:S(2)}) async-start(bf16[8,32,1536]{2,1,0:T(8,128)(2,1)} %bitcast.7), calls=%async_computation.15 | async-start | bytes 1572864 | tf_op jit(solution)/shard_map/all_to_all | solution.py:363
  369.1 12.2 %all-to-all-done.15 = bf16[8,32,1536]{2,1,0:T(8,128)(2,1)} async-done(((bf16[8,32,1536]{2,1,0:T(8,128)(2,1)}), bf16[8,32,1536]{2,1,0:T(8,128)(2,1)}, u32[]{:S(2)}, u32[]{:S(2)}) %all-to-all-start.15) | async-done | bytes 786464 | tf_op jit(solution)/shard_map/all_to_all | solution.py:363
  382.1 4.7 %all-to-all-start.18 = ((bf16[8,112,256]{2,1,0:T(8,128)(2,1)}), bf16[8,112,256]{2,1,0:T(8,128)(2,1)S(1)}, u32[]{:S(2)}, u32[]{:S(2)}) async-start(bf16[8,112,256]{2,1,0:T(8,128)(2,1)} %broadcast_in_dim.55), calls=%async_computation.18 | async-start | bytes 917504 | tf_op jit(solution)/shard_map/all_to_all | solution.py:363
  388.0 7.4 %all-to-all-done.18.parts_ref = bf16[8,112,256]{2,1,0:T(8,128)(2,1)S(1)} async-done(((bf16[8,112,256]{2,1,0:T(8,128)(2,1)}), bf16[8,112,256]{2,1,0:T(8,128)(2,1)S(1)}, u32[]{:S(2)}, u32[]{:S(2)}) %all-to-all-start.18) | async-done | bytes 458784 | tf_op jit(solution)/shard_map/all_to_all | solution.py:363
  396.5 4.4 %all-to-all-start.16 = ((bf16[8,32,1536]{2,1,0:T(8,128)(2,1)}), bf16[8,32,1536]{2,1,0:T(8,128)(2,1)S(1)}, u32[]{:S(2)}, u32[]{:S(2)}) async-start(bf16[8,32,1536]{2,1,0:T(8,128)(2,1)} %broadcast_in_dim.54), calls=%async_computation.16 | async-start | bytes 1572864 | tf_op jit(solution)/shard_map/all_to_all | solution.py:363
  403.0 11.6 %columns_grad.1 = f32[256,1024]{1,0:T(8,128)} custom-call(bf16[16,1024,256]{2,1,0:T(8,128)(2,1)} %get-tuple-element.42.expo_hbm, bf16[16,1024,256]{2,1,0:T(8,128)(2,1)} %get-tuple-element.58.raised_hbm, f32[1024,128]{1,0:T(8,128)S(1)} %copy-done.17, f32[16,256]{1,0:T(8,128)S(1)} %copy-done.35, f32[16,256]{1,0:T(8,128)S(1)} %copy-done.33, ...), custom_call_target="tpu_custom_call" | custom-call | tf_op jit(solution)/shard_map/columns_grad/pallas_call | solution.py:32
  (143 shorter events, 71.9 us)
Async XLA Ops:
  0.6 10.8 %copy-start.18 = (bf16[1024,256]{1,0:T(8,128)(2,1)S(1)}, bf16[1024,256]{1,0:T(8,128)(2,1)}, u32[]{:S(2)}) copy-start(bf16[1024,256]{1,0:T(8,128)(2,1)} %feats_ref.1) | copy-start | bytes 1572868
  2.5 8.9 %copy-start.41 = (s32[4,256]{1,0:T(4,128)S(1)}, s32[4,256]{1,0:T(4,128)}, u32[]{:S(2)}) copy-start(s32[4,256]{1,0:T(4,128)} %mask_ref.1) | copy-start | bytes 12292
  3.8 22.2 %all-to-all-start = ((bf16[16,112,256]{2,1,0:T(8,128)(2,1)}), bf16[16,112,256]{2,1,0:T(8,128)(2,1)S(1)}, u32[]{:S(2)}, u32[]{:S(2)}) async-start(bf16[16,112,256]{2,1,0:T(8,128)(2,1)} %broadcast_in_dim.42), calls=%async_computation | async-start | bytes 1835008 | tf_op jit(solution)/shard_map/all_to_all | solution.py:363
  27.5 32.9 %all-to-all-start.6 = ((bf16[16,272,256]{2,1,0:T(8,128)(2,1)}), bf16[16,272,256]{2,1,0:T(8,128)(2,1)S(1)}, u32[]{:S(2)}, u32[]{:S(2)}) async-start(bf16[16,272,256]{2,1,0:T(8,128)(2,1)} %broadcast_in_dim.46), calls=%async_computation.6 | async-start | bytes 4456448 | tf_op jit(solution)/shard_map/all_to_all | solution.py:363
  38.2 45.4 %copy-start.30 = (bf16[256,256]{1,0:T(8,128)(2,1)}, bf16[256,256]{1,0:T(8,128)(2,1)S(1)}, u32[]{:S(2)}) copy-start(bf16[256,256]{1,0:T(8,128)(2,1)S(1)} %get-tuple-element.52.hidden_ref) | copy-start | bytes 393220
  60.4 23.8 %all-to-all-start.1 = ((f32[8,32,256]{2,1,0:T(8,128)}), f32[8,32,256]{2,1,0:T(8,128)}, u32[]{:S(2)}, u32[]{:S(2)}) async-start(f32[8,32,256]{2,1,0:T(8,128)} %bitcast.1), calls=%async_computation.1 | async-start | bytes 524288 | tf_op jit(solution)/shard_map/all_to_all | solution.py:363
  84.2 26.4 %copy-start.37 = (f32[16,256]{1,0:T(8,128)}, f32[16,256]{1,0:T(8,128)S(1)}, u32[]{:S(2)}) copy-start(f32[16,256]{1,0:T(8,128)S(1)} %get-tuple-element.60.weight_ref) | copy-start | bytes 49156
  84.9 10.0 %all-to-all-start.7 = ((f32[8,16,256]{2,1,0:T(8,128)}), f32[8,16,256]{2,1,0:T(8,128)S(1)}, u32[]{:S(2)}, u32[]{:S(2)}) async-start(f32[8,16,256]{2,1,0:T(8,128)} %broadcast_in_dim.47), calls=%async_computation.7 | async-start | bytes 262144 | tf_op jit(solution)/shard_map/all_to_all | solution.py:363
  95.6 10.7 %all-to-all-start.2 = ((f32[8,32,256]{2,1,0:T(8,128)}), f32[8,32,256]{2,1,0:T(8,128)S(1)}, u32[]{:S(2)}, u32[]{:S(2)}) async-start(f32[8,32,256]{2,1,0:T(8,128)} %broadcast_in_dim.43), calls=%async_computation.2 | async-start | bytes 524288 | tf_op jit(solution)/shard_map/all_to_all | solution.py:363
  107.0 11.0 %all-to-all-start.8 = ((f32[16,16,256]{2,1,0:T(8,128)}), f32[16,16,256]{2,1,0:T(8,128)S(1)}, u32[]{:S(2)}, u32[]{:S(2)}) async-start(f32[16,16,256]{2,1,0:T(8,128)} %broadcast_in_dim.48), calls=%async_computation.8 | async-start | bytes 524288 | tf_op jit(solution)/shard_map/all_to_all | solution.py:363
  110.8 8.8 %copy-start.39 = (f32[8,256]{1,0:T(8,128)}, f32[8,256]{1,0:T(8,128)S(1)}, u32[]{:S(2)}) copy-start(f32[8,256]{1,0:T(8,128)S(1)} %get-tuple-element.50.inv_ref) | copy-start | bytes 24580
  110.8 8.8 %copy-start.25 = (f32[256,256]{1,0:T(8,128)}, f32[256,256]{1,0:T(8,128)S(1)}, u32[]{:S(2)}) copy-start(f32[256,256]{1,0:T(8,128)S(1)} %get-tuple-element.49.unit_ref) | copy-start | bytes 786436
  119.6 4.7 %copy-start.28 = (f32[16,256]{1,0:T(8,128)S(1)}, f32[16,256]{1,0:T(8,128)}, u32[]{:S(2)}) copy-start(f32[16,256]{1,0:T(8,128)} %copy-done.27) | copy-start | bytes 49156
  119.6 30.5 %all-to-all-start.3 = ((bf16[16,256,256]{2,1,0:T(8,128)(2,1)}), bf16[16,256,256]{2,1,0:T(8,128)(2,1)S(1)}, u32[]{:S(2)}, u32[]{:S(2)}) async-start(bf16[16,256,256]{2,1,0:T(8,128)(2,1)} %broadcast_in_dim.44), calls=%async_computation.3 | async-start | bytes 4194304 | tf_op jit(solution)/shard_map/all_to_all | solution.py:363
  195.9 127.1 %copy-start.34 = (f32[16,256]{1,0:T(8,128)}, f32[16,256]{1,0:T(8,128)S(1)}, u32[]{:S(2)}) copy-start(f32[16,256]{1,0:T(8,128)S(1)} %get-tuple-element.63.norm_sum_ref) | copy-start | bytes 49156
  260.7 30.6 %all-to-all-start.11 = ((bf16[16,256,256]{2,1,0:T(8,128)(2,1)}), bf16[16,256,256]{2,1,0:T(8,128)(2,1)}, u32[]{:S(2)}, u32[]{:S(2)}) async-start(bf16[16,256,256]{2,1,0:T(8,128)(2,1)} %copy-done.7), calls=%async_computation.11 | async-start | bytes 4194304 | tf_op jit(solution)/shard_map/all_to_all | solution.py:363
  292.3 24.5 %all-to-all-start.5 = ((bf16[8,256,256]{2,1,0:T(8,128)(2,1)}), bf16[8,256,256]{2,1,0:T(8,128)(2,1)}, u32[]{:S(2)}, u32[]{:S(2)}) async-start(bf16[8,256,256]{2,1,0:T(8,128)(2,1)} %broadcast_in_dim.45), calls=%async_computation.5 | async-start | bytes 2097152 | tf_op jit(solution)/shard_map/all_to_all | solution.py:363
  317.8 21.7 %copy-start.31 = (bf16[256,256]{1,0:T(8,128)(2,1)S(1)}, bf16[256,256]{1,0:T(8,128)(2,1)}, u32[]{:S(2)}) copy-start(bf16[256,256]{1,0:T(8,128)(2,1)} %copy-done.30) | copy-start | bytes 393220
  317.8 20.3 %all-to-all-start.12 = ((bf16[8,256,256]{2,1,0:T(8,128)(2,1)}), bf16[8,256,256]{2,1,0:T(8,128)(2,1)}, u32[]{:S(2)}, u32[]{:S(2)}) async-start(bf16[8,256,256]{2,1,0:T(8,128)(2,1)} %broadcast_in_dim.51), calls=%async_computation.12 | async-start | bytes 2097152 | tf_op jit(solution)/shard_map/all_to_all | solution.py:363
  345.6 17.4 %copy-start.46 = (f32[8,128]{1,0:T(8,128)}, f32[8,128]{1,0:T(8,128)S(1)}, u32[]{:S(2)}) copy-start(f32[8,128]{1,0:T(8,128)S(1)} %get-tuple-element.62) | copy-start | bytes 12292
  345.6 17.4 %copy-start.13 = (bf16[256,1536]{1,0:T(8,128)(2,1)}, bf16[256,1536]{1,0:T(8,128)(2,1)S(1)}, u32[]{:S(2)}) copy-start(bf16[256,1536]{1,0:T(8,128)(2,1)S(1)} %get-tuple-element.54) | copy-start | bytes 2359300
  363.0 18.3 %all-to-all-start.15 = ((bf16[8,32,1536]{2,1,0:T(8,128)(2,1)}), bf16[8,32,1536]{2,1,0:T(8,128)(2,1)}, u32[]{:S(2)}, u32[]{:S(2)}) async-start(bf16[8,32,1536]{2,1,0:T(8,128)(2,1)} %bitcast.7), calls=%async_computation.15 | async-start | bytes 1572864 | tf_op jit(solution)/shard_map/all_to_all | solution.py:363
  382.1 18.8 %copy-start.29 = (f32[16,256]{1,0:T(8,128)S(1)}, f32[16,256]{1,0:T(8,128)}, u32[]{:S(2)}) copy-start(f32[16,256]{1,0:T(8,128)} %copy-done.27) | copy-start | bytes 49156
  382.1 18.8 %copy-start.33 = (f32[16,256]{1,0:T(8,128)S(1)}, f32[16,256]{1,0:T(8,128)}, u32[]{:S(2)}) copy-start(f32[16,256]{1,0:T(8,128)} %copy-done.32) | copy-start | bytes 49156
  382.1 18.8 %copy-start.35 = (f32[16,256]{1,0:T(8,128)S(1)}, f32[16,256]{1,0:T(8,128)}, u32[]{:S(2)}) copy-start(f32[16,256]{1,0:T(8,128)} %copy-done.34) | copy-start | bytes 49156
  382.1 18.8 %copy-start.38 = (f32[16,256]{1,0:T(8,128)S(1)}, f32[16,256]{1,0:T(8,128)}, u32[]{:S(2)}) copy-start(f32[16,256]{1,0:T(8,128)} %copy-done.37) | copy-start | bytes 49156
  382.1 18.8 %copy-start.45 = (f32[1,1024]{1,0:T(1,128)S(1)}, f32[1,1024]{1,0:T(1,128)}, u32[]{:S(2)}) copy-start(f32[1,1024]{1,0:T(1,128)} %copy-done.44) | copy-start | bytes 12292
  382.1 13.3 %all-to-all-start.18 = ((bf16[8,112,256]{2,1,0:T(8,128)(2,1)}), bf16[8,112,256]{2,1,0:T(8,128)(2,1)S(1)}, u32[]{:S(2)}, u32[]{:S(2)}) async-start(bf16[8,112,256]{2,1,0:T(8,128)(2,1)} %broadcast_in_dim.55), calls=%async_computation.18 | async-start | bytes 917504 | tf_op jit(solution)/shard_map/all_to_all | solution.py:363
  396.5 20.8 %all-to-all-start.16 = ((bf16[8,32,1536]{2,1,0:T(8,128)(2,1)}), bf16[8,32,1536]{2,1,0:T(8,128)(2,1)S(1)}, u32[]{:S(2)}, u32[]{:S(2)}) async-start(bf16[8,32,1536]{2,1,0:T(8,128)(2,1)} %broadcast_in_dim.54), calls=%async_computation.16 | async-start | bytes 1572864 | tf_op jit(solution)/shard_map/all_to_all | solution.py:363
  403.0 11.6 %copy-start.47 = (f32[8,128]{1,0:T(8,128)S(1)}, f32[8,128]{1,0:T(8,128)}, u32[]{:S(2)}) copy-start(f32[8,128]{1,0:T(8,128)} %copy-done.46) | copy-start | bytes 12292
  403.0 12.3 %copy-start.12 = (bf16[8,112,256]{2,1,0:T(8,128)(2,1)S(1)}, bf16[8,112,256]{2,1,0:T(8,128)(2,1)}, u32[]{:S(2)}) copy-start(bf16[8,112,256]{2,1,0:T(8,128)(2,1)} %copy-done.11) | copy-start | bytes 1376260
  403.0 14.3 %copy-start.3 = (bf16[256,1024]{1,0:T(8,128)(2,1)S(1)}, bf16[256,1024]{1,0:T(8,128)(2,1)}, u32[]{:S(2)}) copy-start(bf16[256,1024]{1,0:T(8,128)(2,1)} %copy-done.1) | copy-start | bytes 1572868
  (30 other events, 29.0 us)

commit v2 on v1

v2 whole, which is shorter than its diff:
```python
import jax
import jax.numpy as jnp
from jax import lax
from jax.experimental import pallas as pl
from jax.experimental.pallas import tpu as pltpu
from jax.sharding import PartitionSpec as P

ROUNDS = 3
CAP = 256
TEACHER_TEMP = 0.07
STUDENT_TEMP = 0.1
EPS = 1e-06
GRAD_SCALE = 65536.0
INTERPRET = False
f32, bf16 = (jnp.float32, jnp.bfloat16)
VMEM = pl.BlockSpec(memory_space=pltpu.VMEM)
HBM = pl.BlockSpec(memory_space=pl.ANY)
SMEM = pl.BlockSpec(memory_space=pltpu.SMEM)
NT = (((1,), (1,)), ((), ()))
TN = (((0,), (0,)), ((), ()))
EXTRA = 16
HALF = CAP // 2
LINES = CAP + EXTRA


def mm(a, b, dims=None):
    if dims is None:
        return jnp.dot(a, b, preferred_element_type=f32)
    return lax.dot_general(a, b, dims, preferred_element_type=f32)


def call(body, outs, ins, out_specs=None, in_specs=None, scratch=(), name=None):
    outs = tuple(jax.ShapeDtypeStruct(s, d) for s, d in outs)
    return pl.pallas_call(
        body,
        out_shape=outs,
        in_specs=in_specs or [VMEM] * len(ins),
        out_specs=tuple(out_specs or [VMEM] * len(outs)),
        scratch_shapes=list(scratch),
        interpret=INTERPRET,
        name=name,
        compiler_params=pltpu.CompilerParams(vmem_limit_bytes=48 << 20),
    )(*ins)


def iota(shape, dim):
    return lax.broadcasted_iota(jnp.int32, shape, dim)


def copies(pairs, sems):
    return [pltpu.make_async_copy(a, b, sems.at[i]) for i, (a, b) in enumerate(pairs)]


def start_all(peers, make):
    def go(g, _):
        make(g).start()
        return 0

    lax.fori_loop(0, peers, go, 0)


def wait_all(peers, make):
    def go(g, _):
        make(g).wait()
        return 0

    lax.fori_loop(0, peers, go, 0)


def select_body(at_ref, mask_ref, feats_ref, sel_ref, send_hbm, member_ref, mine_ref, unit_ref, pack_ref, sems):
    crops, patches = mask_ref.shape
    mask = mask_ref[...].astype(f32)
    upto = (iota((patches, patches), 0) <= iota((patches, patches), 1)).astype(f32).astype(bf16)
    rank = mm(mask.astype(bf16), upto)
    count = jnp.sum(mask, axis=1, keepdims=True)
    total = jnp.sum(count, axis=0, keepdims=True)
    slot = iota((CAP, patches), 0).astype(f32)
    lane = iota((1, CAP), 1).astype(f32)
    start = jnp.zeros((1, 1), f32)
    weight = jnp.zeros((1, CAP), f32)
    first = iota((CAP, patches), 1) == 0
    member_ref[...] = jnp.zeros_like(member_ref)
    for c in range(crops):
        hit = jnp.where((rank[c : c + 1] + start == slot + 1.0) & (mask[c : c + 1] > 0.0), 1.0, 0.0)
        if c == 0:
            hit = jnp.where(first & (slot >= total), 1.0, hit)
        sel_ref[:, c * patches : (c + 1) * patches] = hit.astype(bf16)
        own = count[c : c + 1]
        inside = jnp.where((lane >= start) & (lane < start + own), 1.0, 0.0)
        part = inside * (1.0 / jnp.maximum(own, 1.0))
        member_ref[c : c + 1, :] = part
        weight = weight + part
        start = start + own
    live = jnp.where(lane < total, 1.0, 0.0)
    picked = mm(sel_ref[...], feats_ref[...])
    scale = lax.rsqrt(jnp.sum(picked * picked, axis=1, keepdims=True) + EPS)
    unit_ref[...] = (picked * scale).astype(bf16)
    at = iota((EXTRA, CAP), 0)
    tail = jnp.where(at == 0, live, jnp.where(at == 1, weight * GRAD_SCALE, 0.0)).astype(bf16)
    mine_ref[...] = tail
    pack_ref[0:HALF, :] = unit_ref[pl.ds(pl.multiple_of(at_ref[0] * HALF, HALF), HALF), :]
    pack_ref[HALF : HALF + EXTRA, :] = tail
    peers = send_hbm.shape[0]
    make = lambda g: pltpu.make_async_copy(pack_ref, send_hbm.at[g], sems.at[g])
    start_all(peers, make)
    wait_all(peers, make)


def columns_body(student_ref, teacher_ref, cols_ref, student_t_ref, teacher_t_ref, norm_ref):
    for part in chunks_of(student_ref.shape[1]):
        wide = student_ref[:, part].astype(f32)
        norm = jnp.sqrt(jnp.sum(wide * wide, axis=0, keepdims=True) + EPS)
        norm_ref[:, part] = norm
        unit = wide / norm
        cols_ref[:, part] = unit.astype(bf16)
        student_t_ref[part, :] = unit.T.astype(bf16)
        wide = teacher_ref[:, part].astype(f32)
        norm = jnp.sqrt(jnp.sum(wide * wide, axis=0, keepdims=True) + EPS)
        teacher_t_ref[part, :] = (wide / norm).T.astype(bf16)


def weights_body(at_ref, w_in_ref, w_out_ref, pack_ref):
    rows, hid = w_in_ref.shape
    half = hid // 2
    bot = w_out_ref.shape[1]
    lines = w_out_ref.shape[0] * bot // half
    pack_ref[0:rows, :] = w_in_ref[:, pl.ds(pl.multiple_of(at_ref[0] * half, half), half)]
    for q in range(half // bot):
        pack_ref[rows : rows + lines, q * bot : (q + 1) * bot] = w_out_ref[q * lines : (q + 1) * lines, :]


def weight_loads(at_ref, w_hbm, w_in_ref, w_out_ref, sems):
    peers = w_hbm.shape[0]
    rows = w_in_ref.shape[0] // peers
    lines = w_hbm.shape[1] - rows
    bot = w_out_ref.shape[1]
    quarters = w_hbm.shape[2] // bot
    pairs = [(w_hbm.at[g, 0:rows, :], w_in_ref.at[g * rows : (g + 1) * rows, :]) for g in range(peers)]
    for i in range(peers // 2):
        for q in range(quarters):
            source = w_hbm.at[at_ref[0] * (peers // 2) + i, rows : rows + lines, q * bot : (q + 1) * bot]
            at = (i * quarters + q) * lines
            pairs.append((source, w_out_ref.at[at : at + lines, :]))
    return copies(pairs, sems)


def forward_body(
    at_ref, sel_ref, tokens_hbm, w_hbm, rows_ref, hidden_ref, slope_ref, feats_ref, tokens_ref, w_in_ref, w_out_ref, sems, tsem
):
    tokens = pltpu.make_async_copy(tokens_hbm, tokens_ref, tsem)
    tokens.start()
    loads = weight_loads(at_ref, w_hbm, w_in_ref, w_out_ref, sems)
    for load in loads:
        load.start()
    tokens.wait()
    rows = mm(sel_ref[...], tokens_ref[...]).astype(bf16)
    rows_ref[...] = rows
    for load in loads:
        load.wait()
    feats = jnp.zeros(feats_ref.shape, f32)
    for part in chunks_of(hidden_ref.shape[1]):
        pre = mm(rows, w_in_ref[:, part])
        cdf = 0.5 * (1.0 + lax.erf(pre * 0.7071067811865476))
        slope_ref[:, part] = cdf + pre * (jnp.exp(-0.5 * pre * pre) * 0.3989422804014327)
        hidden = (pre * cdf).astype(bf16)
        hidden_ref[:, part] = hidden
        feats = feats + mm(hidden, w_out_ref[part, :])
    feats_ref[...] = feats


def unit_body(feats_ref, other_ref, unit_ref, inv_ref, rows_ref):
    feats = feats_ref[...] + other_ref[...]
    inv = lax.rsqrt(jnp.sum(feats * feats, axis=1, keepdims=True) + EPS)
    unit = feats * inv
    unit_ref[...] = unit.T
    inv_ref[...] = jnp.broadcast_to(inv, feats.shape).T[0:8]
    rows_ref[...] = unit.astype(bf16)


def chunks_of(width):
    step = min(256, width)
    return [slice(at, at + step) for at in range(0, width, step)]


def row_of(ref, g):
    return ref[pl.ds(g, 1), :]


def fold(x):
    return x.reshape(x.shape[0] // 8, 8, x.shape[1]).sum(axis=0)


def expo_body(
    at_ref, cols_ref, own_hbm, other_hbm, expo_hbm, part_ref, live_ref, weight_ref,
    own_ref, other_ref, expo_ref, total_ref, sums_ref, sems, own_sems, other_sems,
):
    peers = own_hbm.shape[0]
    width = cols_ref.shape[0]
    load_own = lambda g: pltpu.make_async_copy(own_hbm.at[g], own_ref.at[g], own_sems.at[g])
    load_other = lambda g: pltpu.make_async_copy(other_hbm.at[g], other_ref.at[g], other_sems.at[g])
    store = lambda g: pltpu.make_async_copy(expo_ref.at[g], expo_hbm.at[g], sems.at[g])
    start_all(peers, load_own)
    start_all(peers, load_other)
    total_ref[...] = jnp.zeros_like(total_ref)
    low = at_ref[0] == 0

    def first(g, _):
        load_own(g).wait()
        load_other(g).wait()
        own = own_ref[g, 0:HALF, :]
        other = other_ref[g, 0:HALF, :]
        rows = jnp.concatenate([jnp.where(low, own, other), jnp.where(low, other, own)], axis=0)
        tail = own_ref[g, HALF : HALF + EXTRA, :].astype(f32)
        live = tail[0:1]
        live_ref[pl.ds(g, 1), :] = live
        weight_ref[pl.ds(g, 1), :] = tail[1:2]
        for part in chunks_of(width):
            cos = mm(cols_ref[part, :], rows, NT)
            expo = jnp.exp(cos * (1.0 / TEACHER_TEMP)) * live
            expo_ref[g, part, :] = expo.astype(bf16)
            total_ref[part, :] += expo[:, 0:128] + expo[:, 128:256]
        store(g).start()
        return 0

    lax.fori_loop(0, peers, first, 0)
    spread_scale(total_ref)
    row_parts(expo_ref, total_ref, sums_ref, part_ref)
    wait_all(peers, store)


def spread_scale(total_ref):
    for part in chunks_of(total_ref.shape[0]):
        sums = jnp.sum(total_ref[part, :], axis=1, keepdims=True)
        total_ref[part, :] = jnp.broadcast_to(1.0 / sums, sums.shape[:1] + (128,))


def scaled(expo, scale):
    return jnp.concatenate([expo[:, 0:128] * scale, expo[:, 128:256] * scale], axis=1)


def row_parts(expo_ref, scale_ref, sums_ref, part_ref):
    def step(g, _):
        acc = jnp.zeros((8, CAP), f32)
        for part in chunks_of(scale_ref.shape[0]):
            acc = acc + fold(scaled(expo_ref[g, part, :].astype(f32), scale_ref[part, :]))
        sums_ref[pl.ds(g, 1), :] = jnp.sum(acc, axis=0, keepdims=True)
        return 0

    lax.fori_loop(0, expo_ref.shape[0], step, 0)
    sums = sums_ref[...].astype(bf16)
    for t in range(part_ref.shape[0]):
        part_ref[t] = sums


def relay_body(parts_ref, out_ref):
    sums = parts_ref[0].astype(f32)
    for t in range(1, parts_ref.shape[0]):
        sums = sums + parts_ref[t].astype(f32)
    sums = sums.astype(bf16)
    for g in range(out_ref.shape[0]):
        out_ref[g] = sums


def scales_from(parts_ref, live_ref, scale_ref):
    sums = parts_ref[0].astype(f32)
    for g in range(1, parts_ref.shape[0]):
        sums = sums + parts_ref[g].astype(f32)
    live = live_ref[...]
    scale_ref[...] = live / (sums + 1.0 - live)


def column_sums(load, expo_ref, scale_ref, total_ref):
    total_ref[...] = jnp.zeros_like(total_ref)

    def step(g, _):
        load(g).wait()
        row = row_of(scale_ref, g)
        for part in chunks_of(total_ref.shape[0]):
            expo = expo_ref[g, part, :].astype(f32)
            total_ref[part, :] += expo[:, 0:128] * row[:, 0:128] + expo[:, 128:256] * row[:, 128:256]
        return 0

    lax.fori_loop(0, expo_ref.shape[0], step, 0)
    spread_scale(total_ref)


def balance_body(expo_hbm, parts_ref, live_ref, part_ref, expo_ref, total_ref, sums_ref, scale_ref, sems):
    load = lambda g: pltpu.make_async_copy(expo_hbm.at[g], expo_ref.at[g], sems.at[g])
    start_all(expo_ref.shape[0], load)
    scales_from(parts_ref, live_ref, scale_ref)
    column_sums(load, expo_ref, scale_ref, total_ref)
    row_parts(expo_ref, total_ref, sums_ref, part_ref)


def divide_up(low, g, acc, pull, keep_ref, give_ref):
    rows = jnp.sum(acc, axis=0, keepdims=True)
    rows = jnp.where(iota((EXTRA, CAP), 0) == 0, rows, 0.0).astype(bf16)
    pull = pull.astype(bf16)
    for at, block in ((slice(0, CAP), pull), (slice(CAP, LINES), rows)):
        left, right = (block[:, 0:HALF], block[:, HALF:CAP])
        keep_ref[g, at, :] = jnp.where(low, left, right)
        give_ref[g, at, :] = jnp.where(low, right, left)


def last_body(
    at_ref, expo_hbm, parts_ref, live_ref, cols_ref, keep_hbm, give_hbm, total_ref,
    expo_ref, scale_ref, keep_ref, give_ref, sems, keep_sems, give_sems,
):
    peers = expo_ref.shape[0]
    load = lambda g: pltpu.make_async_copy(expo_hbm.at[g], expo_ref.at[g], sems.at[g])
    keep = lambda g: pltpu.make_async_copy(keep_ref.at[g], keep_hbm.at[g], keep_sems.at[g])
    give = lambda g: pltpu.make_async_copy(give_ref.at[g], give_hbm.at[g], give_sems.at[g])
    start_all(peers, load)
    scales_from(parts_ref, live_ref, scale_ref)
    column_sums(load, expo_ref, scale_ref, total_ref)
    low = at_ref[0] == 0

    def step(g, _):
        acc = jnp.zeros((8, CAP), f32)
        pull = jnp.zeros((cols_ref.shape[0], CAP), f32)
        for part in chunks_of(total_ref.shape[0]):
            balanced = scaled(expo_ref[g, part, :].astype(f32), total_ref[part, :])
            acc = acc + fold(balanced)
            pull = pull + mm(cols_ref[:, part], balanced.astype(bf16))
        divide_up(low, g, acc, pull, keep_ref, give_ref)
        give(g).start()
        keep(g).start()
        return 0

    lax.fori_loop(0, peers, step, 0)
    wait_all(peers, give)
    wait_all(peers, keep)


def student_body(
    at_ref, cols_t_ref, cols_ref, rows_ref, raised_hbm, keep_hbm, give_hbm,
    raised_ref, keep_ref, give_ref, sems, keep_sems, give_sems,
):
    peers = rows_ref.shape[0]
    width = cols_t_ref.shape[0]
    store = lambda g: pltpu.make_async_copy(raised_ref.at[g], raised_hbm.at[g], sems.at[g])
    keep = lambda g: pltpu.make_async_copy(keep_ref.at[g], keep_hbm.at[g], keep_sems.at[g])
    give = lambda g: pltpu.make_async_copy(give_ref.at[g], give_hbm.at[g], give_sems.at[g])
    low = at_ref[0] == 0

    def step(g, _):
        rows = rows_ref[g]
        acc = jnp.zeros((8, CAP), f32)
        pull = jnp.zeros((cols_ref.shape[0], CAP), f32)
        for part in chunks_of(width):
            raised = jnp.exp(mm(cols_t_ref[part, :], rows, NT) * (1.0 / STUDENT_TEMP))
            acc = acc + fold(raised)
            raised = raised.astype(bf16)
            raised_ref[g, part, :] = raised
            pull = pull + mm(cols_ref[:, part], raised)
        divide_up(low, g, acc, pull, keep_ref, give_ref)
        store(g).start()
        give(g).start()
        keep(g).start()
        return 0

    lax.fori_loop(0, peers, step, 0)
    wait_all(peers, give)
    wait_all(peers, keep)
    wait_all(peers, store)


def columns_grad_body(
    expo_hbm, raised_hbm, scale_ref, got_ref, rows_ref, proto_ref, norm_ref,
    grad_ref, expo_ref, raised_ref, acc_ref, esems, rsems,
):
    peers = expo_ref.shape[0]
    load = lambda g: pltpu.make_async_copy(expo_hbm.at[g], expo_ref.at[g], esems.at[g])
    load_raised = lambda g: pltpu.make_async_copy(raised_hbm.at[g], raised_ref.at[g], rsems.at[g])
    start_all(peers, load)
    start_all(peers, load_raised)
    acc_ref[...] = jnp.zeros_like(acc_ref)
    lines = got_ref.shape[1] - EXTRA

    def step(g, _):
        load(g).wait()
        load_raised(g).wait()
        tail = got_ref[g, lines : lines + EXTRA, :].astype(f32)
        alpha = tail[0:1] + tail[1:2]
        beta = tail[2:3] + tail[3:4]
        rows = rows_ref[g]
        for part in chunks_of(acc_ref.shape[0]):
            balanced = scaled(expo_ref[g, part, :].astype(f32), scale_ref[part, :])
            score = raised_ref[g, part, :].astype(f32) * alpha - balanced * beta
            acc_ref[part, :] += mm(score.astype(bf16), rows)
        return 0

    lax.fori_loop(0, peers, step, 0)
    for part in chunks_of(acc_ref.shape[0]):
        grad = acc_ref[part, :].T
        norm = norm_ref[:, part]
        unit = proto_ref[:, part].astype(f32) / norm
        grad_ref[:, part] = (grad - unit * jnp.sum(unit * grad, axis=0, keepdims=True)) / norm


def join(parts_ref):
    halves = []
    for c in range(2):
        acc = parts_ref[c].astype(f32)
        for t in range(c + 2, parts_ref.shape[0], 2):
            acc = acc + parts_ref[t].astype(f32)
        halves.append(acc)
    return jnp.concatenate(halves, axis=1)


def two_parts(x):
    high = x.astype(bf16)
    return (high.astype(f32), x - high.astype(f32))


def backward_body(
    at_ref, push_ref, pull_ref, mine_ref, member_ref, unit_ref, inv_ref, rows_ref, hidden_ref, slope_ref, w_hbm,
    send_hbm, grad_rows_ref, loss_ref, w_in_ref, w_out_ref, send_ref, pre_ref, out_ref, sems, send_sems,
):
    peers = w_hbm.shape[0]
    loads = weight_loads(at_ref, w_hbm, w_in_ref, w_out_ref, sems)
    for load in loads:
        load.start()
    tail = mine_ref[...].astype(f32)
    live, weight = (tail[0:1], tail[1:2] * (1.0 / STUDENT_TEMP))
    push = join(push_ref)
    pull = join(pull_ref)
    norm_sum = push[CAP : CAP + 1]
    push = push[0:CAP]
    scale = live / (pull[CAP : CAP + 1] + 1.0 - live)
    pull = pull[0:CAP]
    unit = unit_ref[...]
    cross = jnp.sum(unit.astype(bf16).astype(f32) * pull, axis=0, keepdims=True) * (1.0 / STUDENT_TEMP)
    row_loss = jnp.log(norm_sum) - scale * cross
    loss = jnp.sum(member_ref[...] * row_loss, axis=1, keepdims=True)
    loss_ref[...] = jnp.broadcast_to(loss, loss_ref.shape)
    alpha = weight / norm_sum
    beta = weight * scale
    grad_unit = push * alpha - pull * beta
    inner = jnp.sum(unit * grad_unit, axis=0, keepdims=True)
    grad_feats = (inv_ref[0:1] * (grad_unit - unit * inner)).T.astype(bf16)
    for load in loads:
        load.wait()
    width = send_ref.shape[2]
    grad_rows = jnp.zeros(grad_rows_ref.shape, f32)
    for part in chunks_of(hidden_ref.shape[1]):
        grad_pre = (mm(grad_feats, w_out_ref[part, :], NT) * slope_ref[:, part]).astype(bf16)
        pre_ref[:, part] = grad_pre
        grad_rows = grad_rows + mm(grad_pre, w_in_ref[:, part], NT)
        out_ref[part, :] = mm(hidden_ref[:, part], grad_feats, TN).astype(bf16)
    grad_rows_ref[...] = grad_rows.astype(bf16)
    core, level = (at_ref[0], at_ref[1])
    own = pre_ref[:, pl.ds(pl.multiple_of(level * width, width), width)]
    grad_in = mm(rows_ref[...], own, TN).astype(bf16)
    per = grad_in.shape[0] // peers
    block = out_ref.shape[0] // (peers // 2)
    share = block // 4
    at = iota((EXTRA, CAP), 0)
    rows = jnp.zeros((EXTRA, CAP), f32)
    for i, x in enumerate(two_parts(alpha) + two_parts(beta)):
        rows = jnp.where(at == i, x, rows)
    rows = rows.astype(bf16)
    store = lambda g: pltpu.make_async_copy(send_ref.at[g], send_hbm.at[g], send_sems.at[g])
    for g in range(peers):
        send_ref[g, 0:per, :] = grad_in[g * per : (g + 1) * per, :]
        start = pl.multiple_of((g % (peers // 2)) * block + level * share, share)
        out = out_ref[pl.ds(start, share), :]
        send_ref[g, per : per + share, :] = jnp.where(core == g // (peers // 2), out, jnp.zeros_like(out))
        send_ref[g, per + share : per + share + EXTRA, :] = rows
        store(g).start()
    wait_all(peers, store)


def place_body(sel_ref, rows_ref, other_ref, out_hbm, out_ref, sems):
    rows = (rows_ref[...].astype(f32) + other_ref[...].astype(f32)).astype(bf16)
    pieces = out_ref.shape[0]
    size = out_ref.shape[1]
    store = lambda i: pltpu.make_async_copy(out_ref.at[i], out_hbm.at[i], sems.at[i])
    for i in range(pieces):
        out_ref[i] = mm(sel_ref[:, i * size : (i + 1) * size], rows, TN).astype(bf16)
        store(i).start()
    wait_all(pieces, store)


def gather_grads_body(got_ref, send_ref):
    peers = got_ref.shape[0]
    lines = send_ref.shape[1]
    acc = got_ref[0, 0:lines, :].astype(f32)
    for g in range(1, peers):
        acc = acc + got_ref[g, 0:lines, :].astype(f32)
    acc = acc.astype(bf16)
    for t in range(send_ref.shape[0]):
        send_ref[t] = acc


def weight_grads_body(at_ref, parts_ref, grad_in_ref, grad_out_ref):
    peers, lines, width = parts_ref.shape
    per = grad_in_ref.shape[0]
    share = lines - per
    for t in range(peers):
        to = ((t % 2) * (peers // 2) + t // 2) * width
        grad_in_ref[:, to : to + width] = parts_ref[t, 0:per, :].astype(f32)
    for z in range(peers // 2):
        grad_out_ref[z * share : (z + 1) * share, :] = parts_ref[2 * z + at_ref[2], per:lines, :].astype(f32)


def exchange(x, axis):
    return lax.all_to_all(x, axis, split_axis=0, concat_axis=0, tiled=True)


def sibling(x):
    peers = lax.axis_size("tensor")
    return lax.ppermute(x, "tensor", [(i, i ^ 1) for i in range(peers)])


def everywhere(part, small):
    got = exchange(part, "tensor")
    (sums,) = call(relay_body, [((small[0], *small), bf16)], (got,), name="relay")
    return exchange(sums, "dp")


def reduced(keep, give):
    both = (keep.astype(f32) + sibling(give).astype(f32)).astype(bf16)
    got = exchange(both, "dp")
    part = got.astype(f32).sum(axis=0).astype(bf16)
    return exchange(jnp.broadcast_to(part, (lax.axis_size("tensor"), *part.shape)), "tensor")


def shards(tokens, teacher_feats, masks, w_in, w_out, proto_student, proto_teacher):
    dim = tokens.shape[1]
    hid = w_in.shape[1]
    bot, width = proto_student.shape
    dp, tensor = (lax.axis_size("dp"), lax.axis_size("tensor"))
    per = w_in.shape[0]
    half = hid // 2
    share = w_out.shape[0] // 4
    t = lax.axis_index("tensor").astype(jnp.int32)
    g = lax.axis_index("dp").astype(jnp.int32)
    at = jnp.stack([t % 2, t // 2, g // (dp // 2)])

    lines = per + w_out.shape[0] * bot // half
    (w_pack,) = call(weights_body, [((lines, half), bf16)], (at, w_in, w_out), in_specs=[SMEM, VMEM, VMEM], name="weights")
    w_all = lax.all_gather(w_pack, "dp", axis=0, tiled=True).reshape(dp, lines, half)
    dma = pltpu.SemaphoreType.DMA
    sems = dma((dp,))
    sel, send, member, mine = call(
        select_body,
        [((CAP, tokens.shape[0]), bf16), ((dp, HALF + EXTRA, bot), bf16), ((8, CAP), f32), ((EXTRA, CAP), bf16)],
        (at, masks, teacher_feats),
        in_specs=[SMEM, VMEM, VMEM],
        out_specs=[VMEM, HBM, VMEM, VMEM],
        scratch=[pltpu.VMEM((CAP, bot), bf16), pltpu.VMEM((HALF + EXTRA, bot), bf16), sems],
        name="select",
    )
    packs = exchange(send, "dp")
    others = sibling(packs)
    cols, student_t, teacher_t, norm = call(
        columns_body,
        [((bot, width), bf16), ((width, bot), bf16), ((width, bot), bf16), ((1, width), f32)],
        (proto_student, proto_teacher),
        name="columns",
    )
    big = ((dp, width, CAP), bf16)
    small = ((dp, CAP), f32)
    part_out = ((tensor, dp, CAP), bf16)
    held = pltpu.VMEM(*big)
    sums = pltpu.VMEM((width, 128), f32)
    pack_held = pltpu.VMEM((dp, HALF + EXTRA, bot), bf16)
    expo, part, live, weight = call(
        expo_body,
        [big, part_out, small, small],
        (at, teacher_t, packs, others),
        in_specs=[SMEM, VMEM, HBM, HBM],
        out_specs=[HBM, VMEM, VMEM, VMEM],
        scratch=[pack_held, pack_held, held, sums, pltpu.VMEM(*small), sems, sems, sems],
        name="expo",
    )
    loads = dma((dp + 2 * dp,))
    w_held = [pltpu.VMEM((dim, half), bf16), pltpu.VMEM((half, bot), bf16)]
    rows, hidden, slope, feats = call(
        forward_body,
        [((CAP, dim), bf16), ((CAP, half), bf16), ((CAP, half), f32), ((CAP, bot), f32)],
        (at, sel, tokens, w_all),
        in_specs=[SMEM, VMEM, HBM, HBM],
        scratch=[pltpu.VMEM(tokens.shape, bf16), *w_held, loads, dma(())],
        name="forward",
    )
    unit, inv, student_rows = call(
        unit_body, [((bot, CAP), f32), ((8, CAP), f32), ((CAP, bot), bf16)], (feats, sibling(feats)), name="unit"
    )
    all_rows = lax.all_gather(student_rows, "dp", axis=0, tiled=True).reshape(dp, CAP, bot)
    got = everywhere(part, small[0])
    (part,) = call(
        balance_body,
        [part_out],
        (expo, got, live),
        in_specs=[HBM, VMEM, VMEM],
        scratch=[held, sums, pltpu.VMEM(*small), pltpu.VMEM(*small), sems],
        name="balance",
    )
    got = everywhere(part, small[0])
    halves = ((dp, LINES, HALF), bf16)
    half_held = pltpu.VMEM(*halves)
    keep, give, scale = call(
        last_body,
        [halves, halves, ((width, 128), f32)],
        (at, expo, got, live, cols),
        in_specs=[SMEM, HBM, VMEM, VMEM, VMEM],
        out_specs=[HBM, HBM, VMEM],
        scratch=[held, pltpu.VMEM(*small), half_held, half_held, sems, sems, sems],
        name="last",
    )
    pull = reduced(keep, give)
    raised, keep, give = call(
        student_body,
        [big, halves, halves],
        (at, student_t, cols, all_rows),
        in_specs=[SMEM, VMEM, VMEM, VMEM],
        out_specs=[HBM, HBM, HBM],
        scratch=[held, half_held, half_held, sems, sems, sems],
        name="student",
    )
    push = reduced(keep, give)
    back_lines = per + share + EXTRA
    send, grad_rows, loss = call(
        backward_body,
        [((dp, back_lines, bot), bf16), ((CAP, dim), bf16), ((8, 128), f32)],
        (at, push, pull, mine, member, unit, inv, rows, hidden, slope, w_all),
        in_specs=[SMEM] + [VMEM] * 9 + [HBM],
        out_specs=[HBM, VMEM, VMEM],
        scratch=[
            *w_held,
            pltpu.VMEM((dp, back_lines, bot), bf16),
            pltpu.VMEM((CAP, half), bf16),
            pltpu.VMEM((half, bot), bf16),
            loads,
            sems,
        ],
        name="backward",
    )
    got = exchange(send, "dp")
    (sent,) = call(gather_grads_body, [((tensor, per + share, bot), bf16)], (got,), name="gather_grads")
    parts = exchange(sent, "tensor")
    (grad_proto,) = call(
        columns_grad_body,
        [((bot, width), f32)],
        (expo, raised, scale, got, all_rows, proto_student, norm),
        in_specs=[HBM, HBM] + [VMEM] * 5,
        scratch=[held, held, pltpu.VMEM((width, bot), f32), sems, sems],
        name="columns_grad",
    )
    pieces = 4
    d_shape = (pieces, tokens.shape[0] // pieces, dim)
    (d_tokens,) = call(
        place_body,
        [(d_shape, bf16)],
        (sel, grad_rows, sibling(grad_rows)),
        out_specs=[HBM],
        scratch=[pltpu.VMEM(d_shape, bf16), dma((pieces,))],
        name="place",
    )
    grad_in, grad_out = call(
        weight_grads_body,
        [((per, hid), f32), ((w_out.shape[0], bot), f32)],
        (at, parts),
        in_specs=[SMEM, VMEM],
        name="weight_grads",
    )
    return (d_tokens.reshape(tokens.shape), grad_in, grad_out, grad_proto, loss[: masks.shape[0], 0])


def solution(mesh):
    placed = (
        P("dp", None),
        P("dp", None),
        P("dp", None),
        P("dp", None),
        P("dp", None),
        P(None, ("dp", "tensor")),
        P(None, ("dp", "tensor")),
    )
    return jax.shard_map(
        shards,
        mesh=mesh,
        in_specs=placed,
        out_specs=(P("dp", None), P("dp", None), P("dp", None), P(None, ("dp", "tensor")), P("dp")),
        check_vma=False,
    )
```

time: 422 us -> 336 us (0.80)
  starting transfers between devices: 71.5 us -> 29.2 us
  waiting for transfers between devices: 142 us -> 111 us
  Pallas kernels: 56.9 us -> 82.4 us
  local copies, waits for them, and re-layouts: 38.3 us -> 14.6 us
  blocking collectives: 97.7 us -> 76.5 us
  between operations: 1.09 us -> 14.4 us
  other arithmetic: 12.9 us -> 6.82 us
    all_to_all x13 -> x5, waiting for transfers between devices: 142 us -> 57.3 us  [exchange(): return lax.all_to_all(x, axis, split_axis=0, concat_axis=0, tiled=True)]
    all_gather x0 -> x2, waiting for transfers between devices: none -> 50.7 us  [the longest x1 50.7 us: shards(): lax.all_gather(w_pack, 'dp', axis=0, tiled=True).reshape(dp, lines, half)]
    all_to_all x13 -> x5, starting transfers between devices: 71.5 us -> 23.7 us  [exchange(): return lax.all_to_all(x, axis, split_axis=0, concat_axis=0, tiled=True)]
    pallas_call x13 -> x16, Pallas kernels: 56.9 us -> 82.4 us  [call(): pl.pallas_call(body, out_shape=outs, in_specs=in_specs or [VMEM] * len(in...]
    all_to_all x6, blocking collectives: 97.7 us -> 76.5 us  [exchange(): return lax.all_to_all(x, axis, split_axis=0, concat_axis=0, tiled=True)]
    unnamed x98 -> x62, local copies, waits for them, and re-layouts: 26.4 us -> 13 us
    reduce_sum x13 -> x2, other arithmetic: 12.9 us -> 1.69 us  [reduced(): part = got.astype(f32).sum(axis=0).astype(bf16)]
    broadcast_in_dim x14 -> x2, local copies, waits for them, and re-layouts: 10.1 us -> 1.02 us  [reduced(): jnp.broadcast_to(part, (lax.axis_size('tensor'), *part.shape))]
  transfers between devices with their start and end apart: 13 -> 12, of which waited for: 11 -> 7; matrix products, arithmetic and copies ran while one was open for 3% -> 2% of each run, Pallas kernels for 8% -> 20%
where the time goes in v2:
time: 336 us; the launch traced here: 335 us
  waiting for transfers between devices  111 us (33%)
  Pallas kernels  82.4 us (25%)
  blocking collectives  76.5 us (23%)
  starting transfers between devices  29.2 us (9%)
  local copies, waits for them, and re-layouts  14.6 us (4%)
  between operations  14.4 us (4%)
  other arithmetic  6.82 us (2%)
    pallas_call x16, Pallas kernels, call(): pl.pallas_call(body, out_shape=outs, in_specs=in_specs or [VMEM] * len(in...  82.4 us
    all_to_all x6, blocking collectives, exchange(): return lax.all_to_all(x, axis, split_axis=0, concat_axis=0, tiled=True)  76.5 us
    all_to_all x5, waiting for transfers between devices, exchange(): return lax.all_to_all(x, axis, split_axis=0, concat_axis=0, tiled=True)  57.3 us
    all_gather x1, waiting for transfers between devices, shards(): lax.all_gather(w_pack, 'dp', axis=0, tiled=True).reshape(dp, lines, half)  50.7 us
    all_to_all x5, starting transfers between devices, exchange(): return lax.all_to_all(x, axis, split_axis=0, concat_axis=0, tiled=True)  23.7 us
    unnamed x62, local copies, waits for them, and re-layouts  13 us
  transfers between devices with their start and end apart: 12, of which 7 were waited for; matrix products, arithmetic and copies ran while one was open for 2% of the time, Pallas kernels for 20%

profile of v2, /device:TPU:1, one launch (start us, length us, event | category | flops | bytes accessed | tf_op | source)
XLA Modules:
  0.0 335.2 jit_solution(8190821921920868047)
XLA Ops:
  11.2 3.1 select.11
  14.3 50.7 %all-gather.3.cloned.1.call-done = bf16[2048,1024]{1,0:T(8,128)(2,1)} async-done(((bf16[128,1024]{1,0:T(8,128)(2,1)}), bf16[2048,1024]{1,0:T(8,128)(2,1)}) %all-gather.3.cloned.1.call-update) | async-done | bytes 4194320 | tf_op jit(solution)/shard_map/all_gather | solution.py:543
  65.0 7.2 %forward.1 = (bf16[256,1536]{1,0:T(8,128)(2,1)S(1)}, bf16[256,1024]{1,0:T(8,128)(2,1)S(1)}, f32[256,1024]{1,0:T(8,128)S(1)}, f32[256,256]{1,0:T(8,128)S(1)}) custom-call(s32[3]{0:T(128)S(1)} %pad_add_fusion.at_ref, bf16[256,1024]{1,0:T(8,128)(2,1)S(1)} %get-tuple-element.34.sel_ref, bf16[1024,1536]{1,0:T(8,128)(2,1)} %tokens_hbm.1, ...), custom_call_target="tpu_custom_call" | custom-call | tf_op jit(solution)/shard_map/forward/pallas_call | solution.py:34
  79.0 24.8 %all_to_all.55.own_hbm = bf16[16,144,256]{2,1,0:T(8,128)(2,1)S(1)} all-to-all(bf16[16,144,256]{2,1,0:T(8,128)(2,1)S(1)} %get-tuple-element.42), channel_id=1, replica_groups=mesh['dp'=16,'tensor'=8] {'dp'}, dimensions={0} | all-to-all | bytes 2359296 | tf_op jit(solution)/shard_map/all_to_all | solution.py:508
  103.8 1.6 collective-permute-start.2
  105.9 2.0 collective-permute-done.2.other_hbm
  107.9 13.7 %expo.1 = (bf16[16,1024,256]{2,1,0:T(8,128)(2,1)}, bf16[8,16,256]{2,1,0:T(8,128)(2,1)S(1)}, f32[16,256]{1,0:T(8,128)S(1)}, f32[16,256]{1,0:T(8,128)}) custom-call(s32[3]{0:T(128)S(1)} %pad_add_fusion.at_ref, bf16[1024,256]{1,0:T(8,128)(2,1)S(1)} %get-tuple-element.41.cols_ref, bf16[16,144,256]{2,1,0:T(8,128)(2,1)S(1)} %all_to_all.55.own_hbm, ...), custom_call_target="tpu_custom_call" | custom-call | tf_op jit(solution)/shard_map/expo/pallas_call | solution.py:34
  121.6 9.4 %all_to_all.56.parts_ref = bf16[8,16,256]{2,1,0:T(8,128)(2,1)S(1)} all-to-all(bf16[8,16,256]{2,1,0:T(8,128)(2,1)S(1)} %get-tuple-element.44), channel_id=1, replica_groups=mesh['dp'=16,'tensor'=8] {'tensor'}, dimensions={0} | all-to-all | bytes 131072 | tf_op jit(solution)/shard_map/all_to_all | solution.py:508
  131.1 9.7 %all_to_all.57.parts_ref = bf16[16,16,256]{2,1,0:T(8,128)(2,1)S(1)} all-to-all(bf16[16,16,256]{2,1,0:T(8,128)(2,1)S(1)} %relay.2), channel_id=1, replica_groups=mesh['dp'=16,'tensor'=8] {'dp'}, dimensions={0} | all-to-all | bytes 262144 | tf_op jit(solution)/shard_map/all_to_all | solution.py:508
  140.7 5.9 %balance.1 = bf16[8,16,256]{2,1,0:T(8,128)(2,1)S(1)} custom-call(bf16[16,1024,256]{2,1,0:T(8,128)(2,1)} %get-tuple-element.43.expo_hbm, bf16[16,16,256]{2,1,0:T(8,128)(2,1)S(1)} %all_to_all.57.parts_ref, f32[16,256]{1,0:T(8,128)S(1)} %get-tuple-element.45.live_ref), custom_call_target="tpu_custom_call" | custom-call | tf_op jit(solution)/shard_map/balance/pallas_call | solution.py:34
  146.7 9.4 %all_to_all.58.parts_ref = bf16[8,16,256]{2,1,0:T(8,128)(2,1)S(1)} all-to-all(bf16[8,16,256]{2,1,0:T(8,128)(2,1)S(1)} %balance.1), channel_id=1, replica_groups=mesh['dp'=16,'tensor'=8] {'tensor'}, dimensions={0} | all-to-all | bytes 131072 | tf_op jit(solution)/shard_map/all_to_all | solution.py:508
  156.1 9.7 %all_to_all.59.parts_ref = bf16[16,16,256]{2,1,0:T(8,128)(2,1)S(1)} all-to-all(bf16[16,16,256]{2,1,0:T(8,128)(2,1)S(1)} %relay.3), channel_id=1, replica_groups=mesh['dp'=16,'tensor'=8] {'dp'}, dimensions={0} | all-to-all | bytes 262144 | tf_op jit(solution)/shard_map/all_to_all | solution.py:508
  165.7 12.2 %last.1 = (bf16[16,272,128]{2,1,0:T(8,128)(2,1)S(1)}, bf16[16,272,128]{2,1,0:T(8,128)(2,1)}, f32[1024,128]{1,0:T(8,128)S(1)}) custom-call(s32[3]{0:T(128)S(1)} %pad_add_fusion.at_ref, bf16[16,1024,256]{2,1,0:T(8,128)(2,1)} %get-tuple-element.43.expo_hbm, bf16[16,16,256]{2,1,0:T(8,128)(2,1)S(1)} %all_to_all.59.parts_ref, ...), custom_call_target="tpu_custom_call" | custom-call | tf_op jit(solution)/shard_map/last/pallas_call | solution.py:34
  178.0 2.2 collective-permute-start.3
  180.3 1.6 copy-done
  182.9 14.5 %student.1 = (bf16[16,1024,256]{2,1,0:T(8,128)(2,1)}, bf16[16,272,128]{2,1,0:T(8,128)(2,1)S(1)}, bf16[16,272,128]{2,1,0:T(8,128)(2,1)}) custom-call(s32[3]{0:T(128)S(1)} %pad_add_fusion.at_ref, bf16[1024,256]{1,0:T(8,128)(2,1)S(1)} %copy-done.18, bf16[256,1024]{1,0:T(8,128)(2,1)S(1)} %get-tuple-element.36.cols_ref, bf16[16,256,256]{2,1,0:T(8,128)(2,1)S(1)} %bitcast.6), custom_call_target="tpu_custom_call" | custom-call | tf_op jit(solution)/shard_map/student/pallas_call | solution.py:34
  198.6 2.5 add_convert_fusion
  201.1 3.8 %all-to-all-start.7 = ((bf16[16,272,128]{2,1,0:T(8,128)(2,1)}), bf16[16,272,128]{2,1,0:T(8,128)(2,1)S(1)}, u32[]{:S(2)}, u32[]{:S(2)}) async-start(bf16[16,272,128]{2,1,0:T(8,128)(2,1)} %add_convert_fusion), calls=%async_computation.7 | async-start | bytes 2228224 | tf_op jit(solution)/shard_map/all_to_all | solution.py:508
  204.9 2.5 add_convert_fusion.1
  207.5 15.3 %all-to-all-done.7 = bf16[16,272,128]{2,1,0:T(8,128)(2,1)S(1)} async-done(((bf16[16,272,128]{2,1,0:T(8,128)(2,1)}), bf16[16,272,128]{2,1,0:T(8,128)(2,1)S(1)}, u32[]{:S(2)}, u32[]{:S(2)}) %all-to-all-start.7) | async-done | bytes 1114144 | tf_op jit(solution)/shard_map/all_to_all | solution.py:508
  222.8 4.1 %all-to-all-start = ((bf16[16,272,128]{2,1,0:T(8,128)(2,1)}), bf16[16,272,128]{2,1,0:T(8,128)(2,1)S(1)}, u32[]{:S(2)}, u32[]{:S(2)}) async-start(bf16[16,272,128]{2,1,0:T(8,128)(2,1)} %add_convert_fusion.1), calls=%async_computation | async-start | bytes 2228224 | tf_op jit(solution)/shard_map/all_to_all | solution.py:508
  227.1 16.2 %all-to-all-done = bf16[16,272,128]{2,1,0:T(8,128)(2,1)S(1)} async-done(((bf16[16,272,128]{2,1,0:T(8,128)(2,1)}), bf16[16,272,128]{2,1,0:T(8,128)(2,1)S(1)}, u32[]{:S(2)}, u32[]{:S(2)}) %all-to-all-start) | async-done | bytes 1114144 | tf_op jit(solution)/shard_map/all_to_all | solution.py:508
  244.4 6.5 %all-to-all-start.8 = ((bf16[8,272,128]{2,1,0:T(8,128)(2,1)}), bf16[8,272,128]{2,1,0:T(8,128)(2,1)S(1)}, u32[]{:S(2)}, u32[]{:S(2)}) async-start(bf16[8,272,128]{2,1,0:T(8,128)(2,1)} %broadcast_in_dim.7), calls=%async_computation.8 | async-start | bytes 1114112 | tf_op jit(solution)/shard_map/all_to_all | solution.py:508
  250.9 1.5 reduce_sum.24
  252.5 8.2 %all-to-all-done.8.pull_ref = bf16[8,272,128]{2,1,0:T(8,128)(2,1)S(1)} async-done(((bf16[8,272,128]{2,1,0:T(8,128)(2,1)}), bf16[8,272,128]{2,1,0:T(8,128)(2,1)S(1)}, u32[]{:S(2)}, u32[]{:S(2)}) %all-to-all-start.8) | async-done | bytes 557088 | tf_op jit(solution)/shard_map/all_to_all | solution.py:508
  260.7 13.5 %all_to_all.60.push_ref = bf16[8,272,128]{2,1,0:T(8,128)(2,1)S(1)} all-to-all(bf16[8,272,128]{2,1,0:T(8,128)(2,1)S(1)} %broadcast_in_dim.6), channel_id=1, replica_groups=mesh['dp'=16,'tensor'=8] {'tensor'}, dimensions={0} | all-to-all | bytes 1114112 | tf_op jit(solution)/shard_map/all_to_all | solution.py:508
  275.4 5.9 %backward.1 = (bf16[16,144,256]{2,1,0:T(8,128)(2,1)}, bf16[256,1536]{1,0:T(8,128)(2,1)S(1)}, f32[8,128]{1,0:T(8,128)S(1)}) custom-call(s32[3]{0:T(128)S(1)} %pad_add_fusion.at_ref, bf16[8,272,128]{2,1,0:T(8,128)(2,1)S(1)} %all_to_all.60.push_ref, bf16[8,272,128]{2,1,0:T(8,128)(2,1)S(1)} %all-to-all-done.8.pull_ref, bf16[16,256]{1,0:T(8,128)(2,1)S(1)} %copy-done.24, ...), custom_call_target="tpu_custom_call" | custom-call | tf_op jit(solution)/shard_map/backward/pallas_call | solution.py:34
  282.8 3.8 %all-to-all-start.9 = ((bf16[16,144,256]{2,1,0:T(8,128)(2,1)}), bf16[16,144,256]{2,1,0:T(8,128)(2,1)S(1)}, u32[]{:S(2)}, u32[]{:S(2)}) async-start(bf16[16,144,256]{2,1,0:T(8,128)(2,1)} %get-tuple-element.56), calls=%async_computation.9 | async-start | bytes 2359296 | tf_op jit(solution)/shard_map/all_to_all | solution.py:508
  287.3 17.7 %all-to-all-done.9.got_ref = bf16[16,144,256]{2,1,0:T(8,128)(2,1)S(1)} async-done(((bf16[16,144,256]{2,1,0:T(8,128)(2,1)}), bf16[16,144,256]{2,1,0:T(8,128)(2,1)S(1)}, u32[]{:S(2)}, u32[]{:S(2)}) %all-to-all-start.9) | async-done | bytes 1179680 | tf_op jit(solution)/shard_map/all_to_all | solution.py:508
  305.9 5.5 %all-to-all-start.10 = ((bf16[8,128,256]{2,1,0:T(8,128)(2,1)}), bf16[8,128,256]{2,1,0:T(8,128)(2,1)S(1)}, u32[]{:S(2)}, u32[]{:S(2)}) async-start(bf16[8,128,256]{2,1,0:T(8,128)(2,1)} %gather_grads.1), calls=%async_computation.10 | async-start | bytes 1048576 | tf_op jit(solution)/shard_map/all_to_all | solution.py:508
  312.0 3.4 %place.1 = bf16[4,256,1536]{2,1,0:T(8,128)(2,1)} custom-call(bf16[256,1024]{1,0:T(8,128)(2,1)S(1)} %get-tuple-element.34.sel_ref, bf16[256,1536]{1,0:T(8,128)(2,1)S(1)} %copy-done.10, bf16[256,1536]{1,0:T(8,128)(2,1)} %collective-permute-done.4.other_ref), custom_call_target="tpu_custom_call" | custom-call | tf_op jit(solution)/shard_map/place/pallas_call | solution.py:34
  315.4 11.5 %columns_grad.1 = f32[256,1024]{1,0:T(8,128)} custom-call(bf16[16,1024,256]{2,1,0:T(8,128)(2,1)} %get-tuple-element.43.expo_hbm, bf16[16,1024,256]{2,1,0:T(8,128)(2,1)} %get-tuple-element.59.raised_hbm, f32[1024,128]{1,0:T(8,128)S(1)} %copy-done.14, bf16[16,144,256]{2,1,0:T(8,128)(2,1)S(1)} %all-to-all-done.9.got_ref, bf16[16,256,256]{2,1,0:T(8,128)(2,1)S(1)} %bitcast.7, ...), custom_call_target="tpu_custom_call" | custom-call | tf_op jit(solution)/shard_map/columns_grad/pallas_call | solution.py:34
  (86 shorter events, 21.1 us)
Async XLA Ops:
  7.2 3.3 copy-start.15
  7.2 57.9 %all-gather.3.cloned.1.call-start = ((), (), s32[]{:S(2)}) async-start(), calls=%async_computation.11 | async-start | bytes 4456448 | tf_op jit(solution)/shard_map/all_gather | solution.py:543
  10.4 169.8 %all-gather.5.cloned.1.call-start = ((), (), s32[]{:S(2)}) async-start(), calls=%async_computation.12 | async-start | bytes 2228224 | tf_op jit(solution)/shard_map/all_gather | solution.py:591
  14.3 57.9 %copy-start.23 = (bf16[16,256]{1,0:T(8,128)(2,1)}, bf16[16,256]{1,0:T(8,128)(2,1)S(1)}, u32[]{:S(2)}) copy-start(bf16[16,256]{1,0:T(8,128)(2,1)S(1)} %get-tuple-element.48.mine_ref) | copy-start | bytes 24580
  74.9 2.0 collective-permute-start
  79.0 26.5 %copy-start.2 = (bf16[256,1024]{1,0:T(8,128)(2,1)S(1)}, bf16[256,1024]{1,0:T(8,128)(2,1)}, u32[]{:S(2)}) copy-start(bf16[256,1024]{1,0:T(8,128)(2,1)} %proto_ref.1) | copy-start | bytes 1572868
  79.0 26.5 %copy-start.16 = (bf16[256,1024]{1,0:T(8,128)(2,1)S(1)}, bf16[256,1024]{1,0:T(8,128)(2,1)}, u32[]{:S(2)}) copy-start(bf16[256,1024]{1,0:T(8,128)(2,1)} %teacher_ref.1) | copy-start | bytes 1572868
  103.8 4.1 %collective-permute-start.2 = (bf16[16,144,256]{2,1,0:T(8,128)(2,1)S(1)}, bf16[16,144,256]{2,1,0:T(8,128)(2,1)S(1)}, u32[]{:S(2)}, u32[]{:S(2)}) collective-permute-start(bf16[16,144,256]{2,1,0:T(8,128)(2,1)S(1)} %all_to_all.55.own_hbm), channel_id=1, source_target_pairs={{0,1},{1,0},{2,3},{3,2},{4,5},{5,4},{6,7},{7,6},{8,9},{9,8},{10,11... | collective-permute-start | bytes 3538952 | tf_op jit(solution)/shard_map/ppermute | solution.py:513
  105.9 15.7 %copy-start.17 = (bf16[1024,256]{1,0:T(8,128)(2,1)}, bf16[1024,256]{1,0:T(8,128)(2,1)S(1)}, u32[]{:S(2)}) copy-start(bf16[1024,256]{1,0:T(8,128)(2,1)S(1)} %get-tuple-element.35.cols_t_ref) | copy-start | bytes 1572868
  178.0 19.4 %copy-start.13 = (f32[1024,128]{1,0:T(8,128)}, f32[1024,128]{1,0:T(8,128)S(1)}, u32[]{:S(2)}) copy-start(f32[1024,128]{1,0:T(8,128)S(1)} %get-tuple-element.60.scale_ref) | copy-start | bytes 1572868
  178.0 20.5 %collective-permute-start.3 = (bf16[16,272,128]{2,1,0:T(8,128)(2,1)}, bf16[16,272,128]{2,1,0:T(8,128)(2,1)}, u32[]{:S(2)}, u32[]{:S(2)}) collective-permute-start(bf16[16,272,128]{2,1,0:T(8,128)(2,1)} %get-tuple-element.47), channel_id=1, source_target_pairs={{0,1},{1,0},{2,3},{3,2},{4,5},{5,4},{6,7},{7,6},{8,9},{9,8},{10,11... | collective-permute-start | bytes 3342344 | tf_op jit(solution)/shard_map/ppermute | solution.py:513
  180.3 1.6 copy-start
  181.8 1.0 copy-start.18
  198.4 6.5 %collective-permute-start.1 = (bf16[16,272,128]{2,1,0:T(8,128)(2,1)}, bf16[16,272,128]{2,1,0:T(8,128)(2,1)}, u32[]{:S(2)}, u32[]{:S(2)}) collective-permute-start(bf16[16,272,128]{2,1,0:T(8,128)(2,1)} %get-tuple-element.40), channel_id=1, source_target_pairs={{0,1},{1,0},{2,3},{3,2},{4,5},{5,4},{6,7},{7,6},{8,9},{9,8},{10,11... | collective-permute-start | bytes 3342344 | tf_op jit(solution)/shard_map/ppermute | solution.py:513
  201.1 3.9 %copy-start.4 = (bf16[16,272,128]{2,1,0:T(8,128)(2,1)S(1)}, bf16[16,272,128]{2,1,0:T(8,128)(2,1)}, u32[]{:S(2)}) copy-start(bf16[16,272,128]{2,1,0:T(8,128)(2,1)} %copy-done.3) | copy-start | bytes 3342340
  201.1 21.7 %all-to-all-start.7 = ((bf16[16,272,128]{2,1,0:T(8,128)(2,1)}), bf16[16,272,128]{2,1,0:T(8,128)(2,1)S(1)}, u32[]{:S(2)}, u32[]{:S(2)}) async-start(bf16[16,272,128]{2,1,0:T(8,128)(2,1)} %add_convert_fusion), calls=%async_computation.7 | async-start | bytes 2228224 | tf_op jit(solution)/shard_map/all_to_all | solution.py:508
  222.8 20.4 %all-to-all-start = ((bf16[16,272,128]{2,1,0:T(8,128)(2,1)}), bf16[16,272,128]{2,1,0:T(8,128)(2,1)S(1)}, u32[]{:S(2)}, u32[]{:S(2)}) async-start(bf16[16,272,128]{2,1,0:T(8,128)(2,1)} %add_convert_fusion.1), calls=%async_computation | async-start | bytes 2228224 | tf_op jit(solution)/shard_map/all_to_all | solution.py:508
  243.2 1.2 copy-start.30
  244.4 16.2 %all-to-all-start.8 = ((bf16[8,272,128]{2,1,0:T(8,128)(2,1)}), bf16[8,272,128]{2,1,0:T(8,128)(2,1)S(1)}, u32[]{:S(2)}, u32[]{:S(2)}) async-start(bf16[8,272,128]{2,1,0:T(8,128)(2,1)} %broadcast_in_dim.7), calls=%async_computation.8 | async-start | bytes 1114112 | tf_op jit(solution)/shard_map/all_to_all | solution.py:508
  250.9 23.3 %copy-start.6 = (f32[256,1024]{1,0:T(8,128)S(1)}, f32[256,1024]{1,0:T(8,128)}, u32[]{:S(2)}) copy-start(f32[256,1024]{1,0:T(8,128)} %copy-done.5) | copy-start | bytes 3145732
  250.9 23.3 %copy-start.12 = (bf16[256,1024]{1,0:T(8,128)(2,1)S(1)}, bf16[256,1024]{1,0:T(8,128)(2,1)}, u32[]{:S(2)}) copy-start(bf16[256,1024]{1,0:T(8,128)(2,1)} %copy-done.11) | copy-start | bytes 1572868
  250.9 23.3 %copy-start.21 = (f32[256,256]{1,0:T(8,128)S(1)}, f32[256,256]{1,0:T(8,128)}, u32[]{:S(2)}) copy-start(f32[256,256]{1,0:T(8,128)} %copy-done.20) | copy-start | bytes 786436
  250.9 23.3 %copy-start.24 = (bf16[16,256]{1,0:T(8,128)(2,1)S(1)}, bf16[16,256]{1,0:T(8,128)(2,1)}, u32[]{:S(2)}) copy-start(bf16[16,256]{1,0:T(8,128)(2,1)} %copy-done.23) | copy-start | bytes 24580
  250.9 23.3 %copy-start.26 = (f32[8,256]{1,0:T(8,128)S(1)}, f32[8,256]{1,0:T(8,128)}, u32[]{:S(2)}) copy-start(f32[8,256]{1,0:T(8,128)} %copy-done.25) | copy-start | bytes 24580
  274.2 1.1 copy-start.8
  282.8 3.8 %copy-start.10 = (bf16[256,1536]{1,0:T(8,128)(2,1)S(1)}, bf16[256,1536]{1,0:T(8,128)(2,1)}, u32[]{:S(2)}) copy-start(bf16[256,1536]{1,0:T(8,128)(2,1)} %copy-done.9) | copy-start | bytes 2359300
  282.8 22.2 %all-to-all-start.9 = ((bf16[16,144,256]{2,1,0:T(8,128)(2,1)}), bf16[16,144,256]{2,1,0:T(8,128)(2,1)S(1)}, u32[]{:S(2)}, u32[]{:S(2)}) async-start(bf16[16,144,256]{2,1,0:T(8,128)(2,1)} %get-tuple-element.56), calls=%async_computation.9 | async-start | bytes 2359296 | tf_op jit(solution)/shard_map/all_to_all | solution.py:508
  286.6 24.7 %copy-start.29 = (f32[8,128]{1,0:T(8,128)S(1)}, f32[8,128]{1,0:T(8,128)}, u32[]{:S(2)}) copy-start(f32[8,128]{1,0:T(8,128)} %copy-done.28) | copy-start | bytes 12292
  286.6 25.3 %collective-permute-start.4 = (bf16[256,1536]{1,0:T(8,128)(2,1)S(1)}, bf16[256,1536]{1,0:T(8,128)(2,1)}, u32[]{:S(2)}, u32[]{:S(2)}) collective-permute-start(bf16[256,1536]{1,0:T(8,128)(2,1)S(1)} %copy-done.10), channel_id=1, source_target_pairs={{0,1},{1,0},{2,3},{3,2},{4,5},{5,4},{6,7},{7,6},{8,9},{9,8},{10,11... | collective-permute-start | bytes 2359304 | tf_op jit(solution)/shard_map/ppermute | solution.py:513
  305.9 21.0 %all-to-all-start.10 = ((bf16[8,128,256]{2,1,0:T(8,128)(2,1)}), bf16[8,128,256]{2,1,0:T(8,128)(2,1)S(1)}, u32[]{:S(2)}, u32[]{:S(2)}) async-start(bf16[8,128,256]{2,1,0:T(8,128)(2,1)} %gather_grads.1), calls=%async_computation.10 | async-start | bytes 1048576 | tf_op jit(solution)/shard_map/all_to_all | solution.py:508
  312.0 3.4 %copy-start.14 = (f32[1024,128]{1,0:T(8,128)S(1)}, f32[1024,128]{1,0:T(8,128)}, u32[]{:S(2)}) copy-start(f32[1024,128]{1,0:T(8,128)} %copy-done.13) | copy-start | bytes 1572868
  312.0 3.4 %copy-start.1 = (bf16[4096,256]{1,0:T(8,128)(2,1)S(1)}, bf16[4096,256]{1,0:T(8,128)(2,1)}, u32[]{:S(2)}) copy-start(bf16[4096,256]{1,0:T(8,128)(2,1)} %all-gather.5.cloned.1.call-done) | copy-start | bytes 6291460
  (11 other events, 8.9 us)
Sparse Core Ops, SparseCore 0:
  10.7 54.2 all-gather.2
  79.1 46.8 all-gather.4
